TPU v7x, 32 devices: a whole 2x2x4 slice. The times are simulated.
32 devices in a mesh: items: 4 (over x, core), rows: 8 (over z, y).
Axes of the slice: x: 2, y: 2, z: 4, core: 2. Of those that a mesh axis runs over, the one named last changes fastest.
Arguments:
- tokens: bfloat16 [16384, 768], P(('items', 'rows')), may hold values from -6 to 6
- query_proj: bfloat16 [768, 768], P(('items', 'rows')), may hold values from -0.21875 to 0.21875
- key_proj: bfloat16 [768, 768], P(('items', 'rows')), may hold values from -0.21875 to 0.21875
- value_proj: bfloat16 [768, 768], P(('items', 'rows')), may hold values from -0.21875 to 0.21875
- query_bias: bfloat16 [768], P(('items', 'rows')), may hold values from -1.5 to 1.5
- value_bias: bfloat16 [768], P(('items', 'rows')), may hold values from -0.25 to 0.25
- output_proj: bfloat16 [768, 768], P(('items', 'rows')), may hold values from -0.875 to 0.875
- output_bias: bfloat16 [768], P(('items', 'rows')), may hold values from -1 to 1
- attn_gain: bfloat16 [768], P(('items', 'rows')), may hold values from 0.099609375 to 1.8984375
- attn_shift: bfloat16 [768], P(('items', 'rows')), may hold values from -1 to 1
- hidden_proj: bfloat16 [768, 3072], P(('items', 'rows')), may hold values from -0.21875 to 0.21875
- hidden_bias: bfloat16 [3072], P(('items', 'rows')), may hold values from -1 to 1
- return_proj: bfloat16 [3072, 768], P(('items', 'rows')), may hold values from -0.109375 to 0.109375
- return_bias: bfloat16 [768], P(('items', 'rows')), may hold values from -1 to 1
- final_gain: bfloat16 [768], P(('items', 'rows')), may hold values from 0.099609375 to 1.8984375
- final_shift: bfloat16 [768], P(('items', 'rows')), may hold values from -2.5 to 2.5
- item_lengths: int32 [4, 8], P('items'), may hold values from 1 to 1024, 4096 in all within a row
- out_grad: bfloat16 [16384, 768], P(('items', 'rows')), may hold values from -6 to 6
Outputs:
- layer_out: bfloat16 [16384, 768], P(('items', 'rows'))
- tokens_grad: float32 [16384, 768], P(('items', 'rows'))
- grad_query_proj: float32 [768, 768], P(('items', 'rows'))
- grad_key_proj: float32 [768, 768], P(('items', 'rows'))
- grad_value_proj: float32 [768, 768], P(('items', 'rows'))
- grad_query_bias: float32 [768], P(('items', 'rows'))
- grad_value_bias: float32 [768], P(('items', 'rows'))
- grad_output_proj: float32 [768, 768], P(('items', 'rows'))
- grad_output_bias: float32 [768], P(('items', 'rows'))
- grad_attn_gain: float32 [768], P(('items', 'rows'))
- grad_attn_shift: float32 [768], P(('items', 'rows'))
- grad_hidden_proj: float32 [768, 3072], P(('items', 'rows'))
- grad_hidden_bias: float32 [3072], P(('items', 'rows'))
- grad_return_proj: float32 [3072, 768], P(('items', 'rows'))
- grad_return_bias: float32 [768], P(('items', 'rows'))
- grad_final_gain: float32 [768], P(('items', 'rows'))
- grad_final_shift: float32 [768], P(('items', 'rows'))
Inputs may be any that keep to these rules, and one draw needn't show every extreme that they name: `item_lengths`: each row lists the lengths of its group's 8 items in stream order and sums to 4096; in each row one item has exactly 1024 tokens.
All inputs are finite; a program needn't handle non-finite values.
Results may differ from a plain program's by a relative error of at most 0.014.
Values may be sent and summed in bfloat16 or wider, within the bound.
A program may use at most 192 MiB of HBM per device.

v0:
```python
import jax
import jax.numpy as jnp
from jax import lax
from jax.sharding import PartitionSpec as P

H = 12
HEAD = 64
REACH = 2
WIN = 2560


eps_norm = 1e-06
masked_score = -1e30


def from_behind(value, axis, by):
    peers = lax.axis_size(axis)
    pairs = [(i, i + by) for i in range(peers) if 0 <= i + by < peers]
    return lax.ppermute(value, axis, pairs)


def dot_plain(matrix, factor):
    return jnp.dot(matrix, factor, preferred_element_type=jnp.float32)


def dot_rows(matrix, factor):
    return lax.dot_general(
        matrix, factor, (((0,), (0,)), ((), ())), preferred_element_type=jnp.float32
    )


def dot_cols(matrix, factor):
    return lax.dot_general(
        matrix, factor, (((1,), (1,)), ((), ())), preferred_element_type=jnp.float32
    )


def layer_norm(hidden, norm_gain, norm_shift):
    row_mean = jnp.mean(hidden, axis=1, keepdims=True)
    centred = hidden - row_mean
    row_var = jnp.mean(centred * centred, axis=1, keepdims=True)
    return centred * lax.rsqrt(row_var + eps_norm) * norm_gain + norm_shift


def gelu_exact(values):
    return jax.nn.gelu(values, approximate=False)


def segment_ids(row_lengths, first_row, num_rows):
    item_ends = jnp.cumsum(row_lengths, dtype=jnp.int32)
    places = first_row + jnp.arange(num_rows, dtype=jnp.int32)
    return jnp.sum(
        (places[:, None] >= item_ends[None, :]).astype(jnp.int32), axis=1, dtype=jnp.int32
    )


def split_heads(values):
    return values.reshape(values.shape[0], H, HEAD).transpose(1, 0, 2)


def join_heads(values):
    return values.transpose(1, 0, 2).reshape(values.shape[1], H * HEAD)


def widen_first(kv_pair):
    pieces = []
    for offset in range(-REACH, REACH + 1):
        if offset == 0:
            pieces.append(kv_pair)
        else:
            pieces.append(from_behind(kv_pair, "rows", -offset))
    return jnp.concatenate(pieces, axis=1)


def widen_again(kv_pair):
    pieces = []
    for offset in range(-REACH, REACH + 1):
        if offset == 0:
            pieces.append(kv_pair)
        else:
            pieces.append(from_behind(kv_pair, "rows", -offset))
    return jnp.concatenate(pieces, axis=1)


def collect(wide_grads):
    rows_dev = wide_grads.shape[1] // (2 * REACH + 1)
    summed = wide_grads[:, REACH * rows_dev : (REACH + 1) * rows_dev]
    for offset in range(-REACH, REACH + 1):
        if offset != 0:
            block_grads = wide_grads[
                :, (offset + REACH) * rows_dev : (offset + REACH + 1) * rows_dev
            ]
            summed = summed + from_behind(block_grads.astype(jnp.bfloat16), "rows", offset).astype(
                block_grads.dtype
            )
    return summed


def attend(query_rows, window, keep_mask):
    score_scale = HEAD ** (-0.5)

    def one_head(head_parts):
        head_query, head_keys, head_values = head_parts
        scores = jnp.where(keep_mask, dot_cols(head_query, head_keys) * score_scale, masked_score)
        row_max = jnp.max(scores, axis=1, keepdims=True)
        lifted = jnp.exp(scores - row_max)
        row_sum = jnp.sum(lifted, axis=1, keepdims=True)
        weights = (lifted / row_sum).astype(jnp.bfloat16)
        return (dot_plain(weights, head_values), (row_max + jnp.log(row_sum))[:, 0])

    outputs, logsum = lax.map(
        one_head, (split_heads(query_rows), split_heads(window[0]), split_heads(window[1]))
    )
    return (join_heads(outputs).astype(jnp.bfloat16), logsum)


def attend_back(query_rows, window, logsum, d_attended, keep_mask):
    score_scale = HEAD ** (-0.5)

    def one_head(head_parts):
        head_query, head_keys, head_values, head_logsum, head_grad = head_parts
        scores = jnp.where(keep_mask, dot_cols(head_query, head_keys) * score_scale, masked_score)
        weights = jnp.exp(scores - head_logsum[:, None])
        d_weights = dot_cols(head_grad, head_values)
        centre = jnp.sum(weights * d_weights, axis=1, keepdims=True)
        d_scores = (weights * (d_weights - centre)).astype(jnp.bfloat16)
        d_head_query = dot_plain(d_scores, head_keys) * score_scale
        d_head_keys = dot_rows(d_scores, head_query) * score_scale
        d_head_values = dot_rows(weights.astype(jnp.bfloat16), head_grad)
        return (d_head_query, d_head_keys, d_head_values)

    d_queries, d_keysets, d_valuesets = lax.map(
        one_head,
        (
            split_heads(query_rows),
            split_heads(window[0]),
            split_heads(window[1]),
            logsum,
            split_heads(d_attended),
        ),
    )
    return (
        join_heads(d_queries).astype(jnp.bfloat16),
        jnp.stack([join_heads(d_keysets), join_heads(d_valuesets)]),
    )


def forward(tokens, params, keep_mask, widen):
    (
        query_proj,
        key_proj,
        value_proj,
        query_bias,
        value_bias,
        output_proj,
        output_bias,
        attn_gain,
        attn_shift,
        hidden_proj,
        hidden_bias,
        return_proj,
        return_bias,
        final_gain,
        final_shift,
    ) = params
    query_rows = (dot_plain(tokens, query_proj) + query_bias.astype(jnp.float32)).astype(
        jnp.bfloat16
    )
    key_rows = dot_plain(tokens, key_proj).astype(jnp.bfloat16)
    value_rows = (dot_plain(tokens, value_proj) + value_bias.astype(jnp.float32)).astype(
        jnp.bfloat16
    )
    window = widen(jnp.stack([key_rows, value_rows]))
    attended, logsum = attend(query_rows, window, keep_mask)
    mixed = tokens.astype(jnp.float32) + (
        dot_plain(attended, output_proj) + output_bias.astype(jnp.float32)
    )
    normed = layer_norm(mixed, attn_gain.astype(jnp.float32), attn_shift.astype(jnp.float32))
    normed_low = normed.astype(jnp.bfloat16)
    hidden_pre = dot_plain(normed_low, hidden_proj) + hidden_bias.astype(jnp.float32)
    active = gelu_exact(hidden_pre).astype(jnp.bfloat16)
    second = normed + (dot_plain(active, return_proj) + return_bias.astype(jnp.float32))
    result = layer_norm(second, final_gain.astype(jnp.float32), final_shift.astype(jnp.float32))
    return (
        result,
        (
            query_rows,
            window,
            logsum,
            attended,
            mixed,
            normed,
            normed_low,
            hidden_pre,
            active,
            second,
        ),
    )


def backward(tokens, params, stored, out_grad, keep_mask):
    (
        query_proj,
        key_proj,
        value_proj,
        query_bias,
        value_bias,
        output_proj,
        output_bias,
        attn_gain,
        attn_shift,
        hidden_proj,
        hidden_bias,
        return_proj,
        return_bias,
        final_gain,
        final_shift,
    ) = params
    query_rows, window, logsum, attended, mixed, normed, normed_low, hidden_pre, active, second = (
        stored
    )
    ignored, final_back = jax.vjp(
        layer_norm, second, final_gain.astype(jnp.float32), final_shift.astype(jnp.float32)
    )
    d_second, grad_final_gain, grad_final_shift = final_back(out_grad.astype(jnp.float32))
    d_ffn = d_second.astype(jnp.bfloat16)
    grad_return_bias = jnp.sum(d_ffn.astype(jnp.float32), axis=0)
    grad_return_proj = dot_rows(active, d_ffn)
    ignored, gelu_back = jax.vjp(gelu_exact, hidden_pre)
    d_hidden = gelu_back(dot_cols(d_ffn, return_proj))[0].astype(jnp.bfloat16)
    grad_hidden_bias = jnp.sum(d_hidden.astype(jnp.float32), axis=0)
    grad_hidden_proj = dot_rows(normed_low, d_hidden)
    d_normed = dot_cols(d_hidden, hidden_proj) + d_second
    ignored, attn_back = jax.vjp(
        layer_norm, mixed, attn_gain.astype(jnp.float32), attn_shift.astype(jnp.float32)
    )
    d_mixed, grad_attn_gain, grad_attn_shift = attn_back(d_normed)
    d_branch = d_mixed.astype(jnp.bfloat16)
    grad_output_bias = jnp.sum(d_branch.astype(jnp.float32), axis=0)
    grad_output_proj = dot_rows(attended, d_branch)
    d_attended = dot_cols(d_branch, output_proj).astype(jnp.bfloat16)
    d_query, wide_grads = attend_back(query_rows, window, logsum, d_attended, keep_mask)
    key_value = collect(wide_grads)
    d_keys = key_value[0].astype(jnp.bfloat16)
    d_values = key_value[1].astype(jnp.bfloat16)
    grad_query_proj = dot_rows(tokens, d_query)
    grad_key_proj = dot_rows(tokens, d_keys)
    grad_value_proj = dot_rows(tokens, d_values)
    grad_query_bias = jnp.sum(d_query.astype(jnp.float32), axis=0)
    grad_value_bias = jnp.sum(d_values.astype(jnp.float32), axis=0)
    tokens_grad = (
        d_mixed
        + dot_cols(d_query, query_proj)
        + dot_cols(d_keys, key_proj)
        + dot_cols(d_values, value_proj)
    )
    return (
        tokens_grad,
        (
            grad_query_proj,
            grad_key_proj,
            grad_value_proj,
            grad_query_bias,
            grad_value_bias,
            grad_output_proj,
            grad_output_bias,
            grad_attn_gain,
            grad_attn_shift,
            grad_hidden_proj,
            grad_hidden_bias,
            grad_return_proj,
            grad_return_bias,
            grad_final_gain,
            grad_final_shift,
        ),
    )


def per_device(
    tokens,
    query_proj,
    key_proj,
    value_proj,
    query_bias,
    value_bias,
    output_proj,
    output_bias,
    attn_gain,
    attn_shift,
    hidden_proj,
    hidden_bias,
    return_proj,
    return_bias,
    final_gain,
    final_shift,
    item_lengths,
    out_grad,
):
    params = (
        lax.all_gather(query_proj, ("items", "rows"), axis=0, tiled=True),
        lax.all_gather(key_proj, ("items", "rows"), axis=0, tiled=True),
        lax.all_gather(value_proj, ("items", "rows"), axis=0, tiled=True),
        lax.all_gather(query_bias, ("items", "rows"), axis=0, tiled=True),
        lax.all_gather(value_bias, ("items", "rows"), axis=0, tiled=True),
        lax.all_gather(output_proj, ("items", "rows"), axis=0, tiled=True),
        lax.all_gather(output_bias, ("items", "rows"), axis=0, tiled=True),
        lax.all_gather(attn_gain, ("items", "rows"), axis=0, tiled=True),
        lax.all_gather(attn_shift, ("items", "rows"), axis=0, tiled=True),
        lax.all_gather(hidden_proj, ("items", "rows"), axis=0, tiled=True),
        lax.all_gather(hidden_bias, ("items", "rows"), axis=0, tiled=True),
        lax.all_gather(return_proj, ("items", "rows"), axis=0, tiled=True),
        lax.all_gather(return_bias, ("items", "rows"), axis=0, tiled=True),
        lax.all_gather(final_gain, ("items", "rows"), axis=0, tiled=True),
        lax.all_gather(final_shift, ("items", "rows"), axis=0, tiled=True),
    )
    rows_dev = tokens.shape[0]
    row_count = lax.axis_size("rows")
    position = lax.axis_index("rows") * rows_dev
    lengths_row = item_lengths[0]
    query_labels = segment_ids(lengths_row, position, rows_dev)
    window_first = position - REACH * rows_dev
    key_labels = segment_ids(lengths_row, window_first, WIN)
    key_places = window_first + jnp.arange(WIN, dtype=jnp.int32)
    inside = (key_places >= 0) & (key_places < row_count * rows_dev)
    keep_mask = (query_labels[:, None] == key_labels[None, :]) & inside[None, :]
    result, stored = forward(tokens, params, keep_mask, widen_first)
    fresh = lax.optimization_barrier((tokens, params, result))
    ignored, stored = forward(fresh[0], fresh[1], keep_mask, widen_again)
    tokens_grad, local_grads = backward(tokens, params, stored, out_grad, keep_mask)
    (
        grad_query_proj,
        grad_key_proj,
        grad_value_proj,
        grad_query_bias,
        grad_value_bias,
        grad_output_proj,
        grad_output_bias,
        grad_attn_gain,
        grad_attn_shift,
        grad_hidden_proj,
        grad_hidden_bias,
        grad_return_proj,
        grad_return_bias,
        grad_final_gain,
        grad_final_shift,
    ) = local_grads
    summed_grads = (
        lax.psum_scatter(grad_query_proj, ("items", "rows"), scatter_dimension=0, tiled=True),
        lax.psum_scatter(grad_key_proj, ("items", "rows"), scatter_dimension=0, tiled=True),
        lax.psum_scatter(grad_value_proj, ("items", "rows"), scatter_dimension=0, tiled=True),
        lax.psum_scatter(grad_query_bias, ("items", "rows"), scatter_dimension=0, tiled=True),
        lax.psum_scatter(grad_value_bias, ("items", "rows"), scatter_dimension=0, tiled=True),
        lax.psum_scatter(grad_output_proj, ("items", "rows"), scatter_dimension=0, tiled=True),
        lax.psum_scatter(grad_output_bias, ("items", "rows"), scatter_dimension=0, tiled=True),
        lax.psum_scatter(grad_attn_gain, ("items", "rows"), scatter_dimension=0, tiled=True),
        lax.psum_scatter(grad_attn_shift, ("items", "rows"), scatter_dimension=0, tiled=True),
        lax.psum_scatter(grad_hidden_proj, ("items", "rows"), scatter_dimension=0, tiled=True),
        lax.psum_scatter(grad_hidden_bias, ("items", "rows"), scatter_dimension=0, tiled=True),
        lax.psum_scatter(grad_return_proj, ("items", "rows"), scatter_dimension=0, tiled=True),
        lax.psum_scatter(grad_return_bias, ("items", "rows"), scatter_dimension=0, tiled=True),
        lax.psum_scatter(grad_final_gain, ("items", "rows"), scatter_dimension=0, tiled=True),
        lax.psum_scatter(grad_final_shift, ("items", "rows"), scatter_dimension=0, tiled=True),
    )
    return (
        result.astype(jnp.bfloat16),
        tokens_grad,
        summed_grads[0],
        summed_grads[1],
        summed_grads[2],
        summed_grads[3],
        summed_grads[4],
        summed_grads[5],
        summed_grads[6],
        summed_grads[7],
        summed_grads[8],
        summed_grads[9],
        summed_grads[10],
        summed_grads[11],
        summed_grads[12],
        summed_grads[13],
        summed_grads[14],
    )


def solution(mesh):
    return jax.shard_map(
        per_device,
        mesh=mesh,
        in_specs=(
            P(("items", "rows"), None),
            P(("items", "rows"), None),
            P(("items", "rows"), None),
            P(("items", "rows"), None),
            P(("items", "rows")),
            P(("items", "rows")),
            P(("items", "rows"), None),
            P(("items", "rows")),
            P(("items", "rows")),
            P(("items", "rows")),
            P(("items", "rows"), None),
            P(("items", "rows")),
            P(("items", "rows"), None),
            P(("items", "rows")),
            P(("items", "rows")),
            P(("items", "rows")),
            P("items", None),
            P(("items", "rows"), None),
        ),
        out_specs=(
            P(("items", "rows"), None),
            P(("items", "rows"), None),
            P(("items", "rows"), None),
            P(("items", "rows"), None),
            P(("items", "rows"), None),
            P(("items", "rows")),
            P(("items", "rows")),
            P(("items", "rows"), None),
            P(("items", "rows")),
            P(("items", "rows")),
            P(("items", "rows")),
            P(("items", "rows"), None),
            P(("items", "rows")),
            P(("items", "rows"), None),
            P(("items", "rows")),
            P(("items", "rows")),
            P(("items", "rows")),
        ),
        check_vma=False,
    )
```

profile of v0, /device:TPU:0, one launch (start us, length us, event | category | flops | bytes accessed | tf_op | source)
XLA Modules:
  0.0 1466.5 jit_solution(15196208716803237145)
XLA Ops:
  18.2 42.3 %all-reduce.19 = (bf16[3072]{0:T(1024)(128)(2,1)S(1)}, bf16[768]{0:T(1024)(128)(2,1)S(1)}, bf16[768]{0:T(1024)(128)(2,1)S(1)}, bf16[768]{0:T(1024)(128)(2,1)S(1)...) all-reduce(bf16[3072]{0:T(1024)(128)(2,1)S(1)} %dynamic-update-slic, ...), channel_id=1, replica_groups=mesh['items'=4,'rows'=8] {'items','rows'}, use_global_device_ids=true, to_apply=%add.5 | all-reduce | flops 9216 | bytes 36864
  70.2 53.8 %all-gather.11.cloned.1.call-done = bf16[768,768]{1,0:T(8,128)(2,1)} async-done(((bf16[24,768]{1,0:T(8,128)(2,1)}), bf16[768,768]{1,0:T(8,128)(2,1)}) %all-gather.11.cloned.1.call-update) | async-done | bytes 1179664 | tf_op jit(solution)/shard_map/all_gather | solution.py:302
  138.7 74.1 %all-gather.7.cloned.1.call-done = bf16[768,768]{1,0:T(8,128)(2,1)} async-done(((bf16[24,768]{1,0:T(8,128)(2,1)}), bf16[768,768]{1,0:T(8,128)(2,1)}) %all-gather.7.cloned.1.call-update) | async-done | bytes 1179664 | tf_op jit(solution)/shard_map/all_gather | solution.py:300
  239.3 65.9 %while.39 = (s32[]{:T(128)}, bf16[12,512,64]{1,2,0:T(8,128)(2,1)S(1)}, bf16[12,512,64]{1,2,0:T(8,128)(2,1)S(1)}, bf16[12,2560,64]{1,2,0:T(8,128)(2,1)}, bf16[12,...) while((s32[]{:T(128)}, ...), condition=%wide.region_6.7_spmd.clone, body=%wide.region_3.6_spmd.clone.sunk | while | flops 348650496 | bytes 16610397 | solution.py:111
  309.0 25.3 %all-gather.15.cloned.1.call-done = bf16[768,3072]{1,0:T(8,128)(2,1)} async-done(((bf16[24,3072]{1,0:T(8,128)(2,1)}), bf16[768,3072]{1,0:T(8,128)(2,1)}) %all-gather.15.cloned.1.call-update) | async-done | bytes 4718608 | tf_op jit(solution)/shard_map/all_gather | solution.py:309
  334.3 64.6 %all-gather.17.cloned.1.call-done = bf16[3072,768]{1,0:T(8,128)(2,1)} async-done(((bf16[96,768]{1,0:T(8,128)(2,1)}), bf16[3072,768]{1,0:T(8,128)(2,1)}) %all-gather.17.cloned.1.call-update) | async-done | bytes 4718608 | tf_op jit(solution)/shard_map/all_gather | solution.py:311
  398.9 22.2 %fusion.146 = (f32[512]{0:T(512)S(1)}, f32[512,768]{1,0:T(8,128)S(1)}) fusion(f32[768]{0:T(1024)S(1)} %convert_element_type.209, bf16[3072,768]{1,0:T(8,128)(2,1)} %all-gather.17.cloned.1.call-done, bf16[768,3072]{1,0:T(8,128)(2,1)} %all-gather.15.cloned.1.call-done, f32[3072]{0:T(1024)S(1)} %convert_element_type.207, f32[512,768]{1,0:T(8,128)} %copy-done.14, ...), kind=kOutput, calls=%fused_computation.239 | convolution fusion | flops 4940365312 | bytes 12610560 | tf_op jit(solution)/shard_map/dot_general | solution.py:23
  439.8 23.6 %collective-permute-done.4 = bf16[2,512,768]{2,1,0:T(8,128)(2,1)} collective-permute-done((bf16[2,512,768]{2,1,0:T(8,128)(2,1)}, bf16[2,512,768]{2,1,0:T(8,128)(2,1)}, u32[]{:S(2)}, u32[]{:S(2)}) %collective-permute-start.4) | collective-permute-done | bytes 1572896 | tf_op jit(solution)/shard_map/ppermute | solution.py:19
  464.9 36.5 %collective-permute-done.5 = bf16[2,512,768]{2,1,0:T(8,128)(2,1)} collective-permute-done((bf16[2,512,768]{2,1,0:T(8,128)(2,1)}, bf16[2,512,768]{2,1,0:T(8,128)(2,1)}, u32[]{:S(2)}, u32[]{:S(2)}) %collective-permute-start.5) | collective-permute-done | bytes 1572896 | tf_op jit(solution)/shard_map/ppermute | solution.py:19
  516.3 8.2 copy.95
  530.7 8.3 copy.96
  539.0 115.3 %while.40 = (s32[]{:T(128)}, bf16[12,512,64]{1,2,0:T(8,128)(2,1)S(1)}, f32[12,512]{1,0:T(8,128)S(1)}, bf16[12,512,64]{2,1,0:T(8,128)(2,1)S(1)}, bf16[12,2560,64]...) while((s32[]{:T(128)}, ...), condition=%wide.region_14.15_spmd.clone, body=%wide.region_11.14_spmd.clone.sunk | while | flops 348651008 | bytes 38313100 | solution.py:111
  657.8 19.9 %multiply_convert_fusion.1 = (bf16[512,3072]{1,0:T(8,128)(2,1)S(1)}, f32[512,3072]{1,0:T(8,128)}, f32[512,3072]{1,0:T(8,128)}) fusion(f32[3072]{0:T(1024)S(1)} %convert_element_type.226, bf16[768,3072]{1,0:T(8,128)(2,1)} %all-gather.15.cloned.1.call-done, f32[512,768]{1,0:T(8,128)S(1)} %get-tuple-element.516, f32[768]{0:T(1024)S(1)} %convert_element_type.224, ...), kind=kOutput, calls=%fused_computation.79 | convolution fusion | flops 2521694208 | bytes 22042624 | tf_op jit(solution)/shard_map/dot_general | solution.py:23
  682.6 8.3 convert_reduce_fusion
  702.8 151.1 %while.41 = (s32[]{:T(128)}, bf16[12,512,64]{1,2,0:T(8,128)(2,1)S(1)}, f32[12,2560,64]{1,2,0:T(8,128)}, f32[12,2560,64]{1,2,0:T(8,128)}, bf16[12,512,64]{2,1,0:T...) while((s32[]{:T(128)}, ...), condition=%wide.region_25.26_spmd.clone, body=%wide.region_23.25_spmd.clone.sunk | while | flops 853474816 | bytes 43153024 | solution.py:132
  859.3 9.8 fusion.56
  880.7 32.6 %collective-permute-done.10 = bf16[2,512,768]{1,2,0:T(8,128)(2,1)S(1)} collective-permute-done((bf16[2,512,768]{1,2,0:T(8,128)(2,1)S(1)}, bf16[2,512,768]{1,2,0:T(8,128)(2,1)S(1)}, u32[]{:S(2)}, u32[]{:S(2)}) %collective-permute-start.10) | collective-permute-done | bytes 1572896 | tf_op jit(solution)/shard_map/ppermute | solution.py:19
  936.0 8.4 fusion.153
  944.5 8.9 fusion.133
  958.5 76.1 %all-reduce.18 = (f32[768]{0:T(1024)S(1)}, f32[768]{0:T(1024)S(1)}, f32[768]{0:T(1024)S(1)}, f32[768]{0:T(1024)S(1)}, f32[768]{0:T(1024)S(1)}, /*index=5*/f32[30...) all-reduce(f32[768]{0:T(1024)S(1)} %reduce_sum.291, ...), channel_id=5, replica_groups=mesh['items'=4,'rows'=8] {'items','rows'}, use_global_device_ids=true, to_apply=%region_30.31.clone | all-reduce | flops 9216 | bytes 73728
  1044.3 27.4 %reduce-scatter.21.cloned.1.call-done = f32[24,768]{1,0:T(8,128)} async-done(((f32[768,768]{1,0:T(8,128)}), f32[24,768]{1,0:T(8,128)}) %reduce-scatter.21.cloned.1.call-update) | async-done | bytes 73744
  1071.6 104.4 %reduce-scatter.23.cloned.1.call-done = f32[24,768]{1,0:T(8,128)} async-done(((f32[768,768]{1,0:T(8,128)}), f32[24,768]{1,0:T(8,128)}) %reduce-scatter.23.cloned.1.call-update) | async-done | bytes 73744
  1176.0 141.8 %reduce-scatter.17.cloned.1.call-done = f32[96,768]{1,0:T(8,128)} async-done(((f32[3072,768]{1,0:T(8,128)}), f32[96,768]{1,0:T(8,128)}) %reduce-scatter.17.cloned.1.call-update) | async-done | bytes 294928 | tf_op jit(solution)/shard_map/reduce_scatter | solution.py:359
  1317.8 141.5 %reduce-scatter.15.cloned.1.call-done = f32[24,3072]{1,0:T(8,128)} async-done(((f32[768,3072]{1,0:T(8,128)}), f32[24,3072]{1,0:T(8,128)}) %reduce-scatter.15.cloned.1.call-update) | async-done | bytes 294928 | tf_op jit(solution)/shard_map/reduce_scatter | solution.py:357
  (432 shorter events, 511.6 us)
Async XLA Ops:
  7.2 60.7 %all-gather.9.cloned.1.call-start = ((), (), s32[]{:S(2)}) async-start(), calls=%async_computation.7 | async-start | bytes 1216512 | tf_op jit(solution)/shard_map/all_gather | solution.py:301
  7.9 116.1 %all-gather.11.cloned.1.call-start = ((), (), s32[]{:S(2)}) async-start(), calls=%async_computation.8 | async-start | bytes 1216512 | tf_op jit(solution)/shard_map/all_gather | solution.py:302
  8.7 204.1 %all-gather.7.cloned.1.call-start = ((), (), s32[]{:S(2)}) async-start(), calls=%async_computation.6 | async-start | bytes 1216512 | tf_op jit(solution)/shard_map/all_gather | solution.py:300
  9.4 295.9 %all-gather.13.cloned.1.call-start = ((), (), s32[]{:S(2)}) async-start(), calls=%async_computation.9 | async-start | bytes 1216512 | tf_op jit(solution)/shard_map/all_gather | solution.py:305
  10.0 324.3 %all-gather.15.cloned.1.call-start = ((), (), s32[]{:S(2)}) async-start(), calls=%async_computation.10 | async-start | bytes 4866048 | tf_op jit(solution)/shard_map/all_gather | solution.py:309
  10.6 388.3 %all-gather.17.cloned.1.call-start = ((), (), s32[]{:S(2)}) async-start(), calls=%async_computation.11 | async-start | bytes 4866048 | tf_op jit(solution)/shard_map/all_gather | solution.py:311
  127.4 89.8 %collective-permute-start = (bf16[2,512,768]{2,1,0:T(8,128)(2,1)}, bf16[2,512,768]{2,1,0:T(8,128)(2,1)}, u32[]{:S(2)}, u32[]{:S(2)}) collective-permute-start(bf16[2,512,768]{2,1,0:T(8,128)(2,1)} %pad_maximum_fusion.1), channel_id=1, source_target_pairs={{0,2},{1,3},{2,4},{3,5},{4,6},{5,7},{8,10},{9,11},{10,12},{11,13},... | collective-permute-start | bytes 4718600 | tf_op jit(solution)/shard_map/ppermute | solution.py:19
  131.0 87.7 %collective-permute-start.1 = (bf16[2,512,768]{2,1,0:T(8,128)(2,1)}, bf16[2,512,768]{2,1,0:T(8,128)(2,1)}, u32[]{:S(2)}, u32[]{:S(2)}) collective-permute-start(bf16[2,512,768]{2,1,0:T(8,128)(2,1)} %pad_maximum_fusion.1), channel_id=1, source_target_pairs={{0,1},{1,2},{2,3},{3,4},{4,5},{5,6},{6,7},{8,9},{9,10},{10,11},{11... | collective-permute-start | bytes 4718600 | tf_op jit(solution)/shard_map/ppermute | solution.py:19
  135.5 84.8 %collective-permute-start.2 = (bf16[2,512,768]{2,1,0:T(8,128)(2,1)}, bf16[2,512,768]{2,1,0:T(8,128)(2,1)}, u32[]{:S(2)}, u32[]{:S(2)}) collective-permute-start(bf16[2,512,768]{2,1,0:T(8,128)(2,1)} %pad_maximum_fusion.1), channel_id=1, source_target_pairs={{1,0},{2,1},{3,2},{4,3},{5,4},{6,5},{7,6},{9,8},{10,9},{11,10},{12... | collective-permute-start | bytes 4718600 | tf_op jit(solution)/shard_map/ppermute | solution.py:19
  136.8 85.0 %collective-permute-start.3 = (bf16[2,512,768]{2,1,0:T(8,128)(2,1)}, bf16[2,512,768]{2,1,0:T(8,128)(2,1)}, u32[]{:S(2)}, u32[]{:S(2)}) collective-permute-start(bf16[2,512,768]{2,1,0:T(8,128)(2,1)} %pad_maximum_fusion.1), channel_id=1, source_target_pairs={{2,0},{3,1},{4,2},{5,3},{6,4},{7,5},{10,8},{11,9},{12,10},{13,11},... | collective-permute-start | bytes 4718600 | tf_op jit(solution)/shard_map/ppermute | solution.py:19
  138.1 906.1 %reduce-scatter.13.cloned.1.call-start = ((), (), s32[]{:S(2)}) async-start(), calls=%async_computation.12 | async-start | bytes 2433024 | tf_op jit(solution)/shard_map/reduce_scatter | solution.py:353
  425.7 37.7 %collective-permute-start.4 = (bf16[2,512,768]{2,1,0:T(8,128)(2,1)}, bf16[2,512,768]{2,1,0:T(8,128)(2,1)}, u32[]{:S(2)}, u32[]{:S(2)}) collective-permute-start(bf16[2,512,768]{2,1,0:T(8,128)(2,1)} %pad_maximum_fusion.2), channel_id=1, source_target_pairs={{0,2},{1,3},{2,4},{3,5},{4,6},{5,7},{8,10},{9,11},{10,12},{11,13},... | collective-permute-start | bytes 4718600 | tf_op jit(solution)/shard_map/ppermute | solution.py:19
  430.2 71.2 %collective-permute-start.5 = (bf16[2,512,768]{2,1,0:T(8,128)(2,1)}, bf16[2,512,768]{2,1,0:T(8,128)(2,1)}, u32[]{:S(2)}, u32[]{:S(2)}) collective-permute-start(bf16[2,512,768]{2,1,0:T(8,128)(2,1)} %pad_maximum_fusion.2), channel_id=1, source_target_pairs={{0,1},{1,2},{2,3},{3,4},{4,5},{5,6},{6,7},{8,9},{9,10},{10,11},{11... | collective-permute-start | bytes 4718600 | tf_op jit(solution)/shard_map/ppermute | solution.py:19
  434.7 68.4 %collective-permute-start.6 = (bf16[2,512,768]{2,1,0:T(8,128)(2,1)}, bf16[2,512,768]{2,1,0:T(8,128)(2,1)}, u32[]{:S(2)}, u32[]{:S(2)}) collective-permute-start(bf16[2,512,768]{2,1,0:T(8,128)(2,1)} %pad_maximum_fusion.2), channel_id=1, source_target_pairs={{1,0},{2,1},{3,2},{4,3},{5,4},{6,5},{7,6},{9,8},{10,9},{11,10},{12... | collective-permute-start | bytes 4718600 | tf_op jit(solution)/shard_map/ppermute | solution.py:19
  436.0 69.2 %collective-permute-start.7 = (bf16[2,512,768]{2,1,0:T(8,128)(2,1)}, bf16[2,512,768]{2,1,0:T(8,128)(2,1)}, u32[]{:S(2)}, u32[]{:S(2)}) collective-permute-start(bf16[2,512,768]{2,1,0:T(8,128)(2,1)} %pad_maximum_fusion.2), channel_id=1, source_target_pairs={{2,0},{3,1},{4,2},{5,3},{6,4},{7,5},{10,8},{11,9},{12,10},{13,11},... | collective-permute-start | bytes 4718600 | tf_op jit(solution)/shard_map/ppermute | solution.py:19
  697.4 346.8 %reduce-scatter.19.cloned.1.call-start = ((), (), s32[]{:S(2)}) async-start(), calls=%async_computation.15 | async-start | bytes 2433024
  859.3 212.3 %reduce-scatter.21.cloned.1.call-start = ((), (), s32[]{:S(2)}) async-start(), calls=%async_computation.16 | async-start | bytes 2433024
  872.5 40.8 %collective-permute-start.10 = (bf16[2,512,768]{1,2,0:T(8,128)(2,1)S(1)}, bf16[2,512,768]{1,2,0:T(8,128)(2,1)S(1)}, u32[]{:S(2)}, u32[]{:S(2)}) collective-permute-start(bf16[2,512,768]{1,2,0:T(8,128)(2,1)S(1)} %get-tuple-element.505), channel_id=1, source_target_pairs={{0,1},{1,2},{2,3},{3,4},{4,5},{5,6},{6,7},{8,9},{9,10},{10,11},{11... | collective-permute-start | bytes 4718600 | tf_op jit(solution)/shard_map/ppermute | solution.py:19
  876.4 37.2 %collective-permute-start.11 = (bf16[2,512,768]{1,2,0:T(8,128)(2,1)S(1)}, bf16[2,512,768]{1,2,0:T(8,128)(2,1)S(1)}, u32[]{:S(2)}, u32[]{:S(2)}) collective-permute-start(bf16[2,512,768]{1,2,0:T(8,128)(2,1)S(1)} %get-tuple-element.504), channel_id=1, source_target_pairs={{0,2},{1,3},{2,4},{3,5},{4,6},{5,7},{8,10},{9,11},{10,12},{11,13},... | collective-permute-start | bytes 4718600 | tf_op jit(solution)/shard_map/ppermute | solution.py:19
  877.9 42.8 %collective-permute-start.8 = (bf16[2,512,768]{1,2,0:T(8,128)(2,1)S(1)}, bf16[2,512,768]{1,2,0:T(8,128)(2,1)S(1)}, u32[]{:S(2)}, u32[]{:S(2)}) collective-permute-start(bf16[2,512,768]{1,2,0:T(8,128)(2,1)S(1)} %get-tuple-element.503), channel_id=1, source_target_pairs={{2,0},{3,1},{4,2},{5,3},{6,4},{7,5},{10,8},{11,9},{12,10},{13,11},... | collective-permute-start | bytes 4718600 | tf_op jit(solution)/shard_map/ppermute | solution.py:19
  879.3 41.5 %collective-permute-start.9 = (bf16[2,512,768]{1,2,0:T(8,128)(2,1)S(1)}, bf16[2,512,768]{1,2,0:T(8,128)(2,1)S(1)}, u32[]{:S(2)}, u32[]{:S(2)}) collective-permute-start(bf16[2,512,768]{1,2,0:T(8,128)(2,1)S(1)} %get-tuple-element.506), channel_id=1, source_target_pairs={{1,0},{2,1},{3,2},{4,3},{5,4},{6,5},{7,6},{9,8},{10,9},{11,10},{12... | collective-permute-start | bytes 4718600 | tf_op jit(solution)/shard_map/ppermute | solution.py:19
  929.2 246.8 %reduce-scatter.23.cloned.1.call-start = ((), (), s32[]{:S(2)}) async-start(), calls=%async_computation.17 | async-start | bytes 2433024
  935.7 382.0 %reduce-scatter.17.cloned.1.call-start = ((), (), s32[]{:S(2)}) async-start(), calls=%async_computation.14 | async-start | bytes 9732096 | tf_op jit(solution)/shard_map/reduce_scatter | solution.py:359
  944.5 514.8 %reduce-scatter.15.cloned.1.call-start = ((), (), s32[]{:S(2)}) async-start(), calls=%async_computation.13 | async-start | bytes 9732096 | tf_op jit(solution)/shard_map/reduce_scatter | solution.py:357
  (38 other events, 587.8 us)
Sparse Core Ops, SparseCore 0:
  10.9 56.9 all-gather.8
  70.8 53.1 all-gather.10
  127.0 85.7 all-gather.6
  215.6 53.3 all-gather.12
  271.7 62.5 all-gather.14
  337.0 61.8 all-gather.16
  697.6 97.2 reduce-scatter.12
  859.4 107.5 reduce-scatter.18
  972.9 98.6 reduce-scatter.20
  1077.3 98.6 reduce-scatter.22
  1182.5 135.2 reduce-scatter.16
  1324.1 135.1 reduce-scatter.14
where the time goes:
time: 1480 us; the launch traced here: 1470 us
  waiting for transfers between devices  744 us (50%)
  matrix products  385 us (26%)
  local copies, waits for them, and re-layouts  121 us (8%)
  blocking collectives  118 us (8%)
  other arithmetic  49.4 us (3%)
  starting transfers between devices  31.2 us (2%)
  between operations  15.6 us (1%)
    dot_general x47, matrix products, dot_plain(): return jnp.dot(matrix, factor, preferred_element_type=jnp.float32)  155 us
    dot_general x54, matrix products, dot_cols(): lax.dot_general(matrix, factor, (((1,), (1,)), ((), ())), preferred_eleme...  148 us
    reduce_scatter x1, waiting for transfers between devices, per_device(): lax.psum_scatter(grad_return_proj, ('items', 'rows'), scatter_dimension=0...  142 us
    reduce_scatter x1, waiting for transfers between devices, per_device(): lax.psum_scatter(grad_hidden_proj, ('items', 'rows'), scatter_dimension=0...  141 us
    unnamed x15, waiting for transfers between devices  135 us
    unnamed x2, blocking collectives  118 us
    ppermute x12, waiting for transfers between devices, from_behind(): return lax.ppermute(value, axis, pairs)  101 us
    dot_general x30, matrix products, dot_rows(): lax.dot_general(matrix, factor, (((0,), (0,)), ((), ())), preferred_eleme...  82.9 us
  transfers between devices with their start and end apart: 24, of which 15 were waited for; matrix products, arithmetic and copies ran while one was open for 23% of the time, Pallas kernels for 0%

commit v1 on v0

v1 whole, which is shorter than its diff:
```python
import functools
import jax
import jax.numpy as jnp
from jax import lax
from jax.experimental import pallas as pl
from jax.experimental.pallas import tpu as pltpu

from jax.sharding import PartitionSpec as P

MESH = pl.DeviceIdType.MESH
REACH = 2


def split_rows(rows):
    inner = 1
    while (2 * inner) ** 2 <= rows:
        inner *= 2
    return rows // inner, inner


def place(nz, ny):
    item, row = lax.axis_index("items"), lax.axis_index("rows")
    return item // 2, item % 2, row // ny, row % ny


def near(z, step, nz):
    way = 1 - 2 * (z // ((nz + 1) // 2))
    return lax.rem(z + way * step + nz * 2, nz)


def gather_kernel(na, nz, ny, count, *refs):
    tokens = refs[0]
    mine = refs[1 : 1 + count]
    window = refs[1 + count]
    full = refs[2 + count : 2 + 2 * count]
    (halo_send, halo_recv, local_sem, s1, r1, s2, r2, s3, r3, s4, r4) = refs[2 + 2 * count :]
    a, c, z, y = place(nz, ny)
    rows = nz * ny
    row = z * ny + y
    item = a * 2 + c

    def slot(a_, z_, y_):
        return (a_ * 2 + c) * rows + z_ * ny + y_

    barrier = pltpu.get_barrier_semaphore()

    def greet(i_, r_):
        pl.semaphore_signal(barrier, inc=1, device_id=(i_, r_), device_id_type=MESH)

    for d in range(1, nz):
        greet(item, near(z, d, nz) * ny + y)
    for d in range(1, ny):
        greet(item, z * ny + lax.rem(y + d, ny))
    for d in range(1, na):
        greet(lax.rem(a + d, na) * 2 + c, row)
    greet(a * 2 + 1 - c, row)
    for d in range(-REACH, REACH + 1):
        if d != 0:
            greet(item, lax.rem(row + d + rows, rows))
    pl.semaphore_wait(barrier, nz + ny + na - 2 + 2 * REACH)

    def remote(src, dst, send, recv, i_, r_):
        return pltpu.make_async_remote_copy(
            src_ref=src, dst_ref=dst, send_sem=send, recv_sem=recv, device_id=(i_, r_), device_id_type=MESH
        )

    locals_ = []
    for n in range(count):
        locals_.append(pltpu.make_async_copy(mine[n], full[n].at[slot(a, z, y)], local_sem.at[n]))
        locals_[-1].start()
    locals_.append(pltpu.make_async_copy(tokens, window.at[REACH], local_sem.at[count]))
    locals_[-1].start()

    for d in range(1, nz):
        zz = near(z, d, nz)
        for n in range(count):
            remote(mine[n], full[n].at[slot(a, z, y)], s1.at[d, n], r1.at[z, n], item, zz * ny + y).start()

    def wait1(zz, n):
        part = full[n].at[slot(a, zz, y)]
        remote(part, part, s1.at[0, n], r1.at[zz, n], item, row).wait_recv()

    def halo(d, start):
        k = d + REACH

        @pl.when((row + d >= 0) & (row + d < rows))
        def _():
            copy = remote(tokens, window.at[REACH - d], halo_send.at[k], halo_recv.at[REACH - d], item, row + d)
            if start:
                copy.start()
            else:
                copy.wait_send()
                part = window.at[k]
                remote(part, part, halo_send.at[k], halo_recv.at[k], item, row).wait_recv()

        @pl.when((row + d < 0) | (row + d >= rows))
        def _():
            copy = pltpu.make_async_copy(tokens, window.at[k], halo_recv.at[k])
            if start:
                copy.start()
            else:
                copy.wait()

    @pl.when(c == 0)
    def _():
        def second(step):
            zz = near(z, step, nz)
            for n in range(count):
                if step:
                    wait1(zz, n)
                for d in range(1, ny):
                    src = full[n].at[slot(a, zz, y)] if step else mine[n]
                    remote(src, full[n].at[slot(a, zz, y)], s2.at[step, d, n], r2.at[zz, y, n], item, z * ny + lax.rem(y + d, ny)).start()

        def third(step):
            zz = near(z, step, nz)
            for n in range(count):
                for d in range(1, ny):
                    yy = lax.rem(y + d, ny)
                    part = full[n].at[slot(a, zz, yy)]
                    remote(part, part, s2.at[step, 0, n], r2.at[zz, yy, n], item, row).wait_recv()
                if step == 0:
                    locals_[n].wait()
                block = full[n].at[pl.ds(slot(a, zz, 0), ny)]
                for d in range(1, na):
                    remote(block, block, s3.at[step, d, 0, n], r3.at[zz, a, 0, n], lax.rem(a + d, na) * 2 + c, row).start()

        def fourth(step):
            zz = near(z, step, nz)
            for e in range(na):
                aa = lax.rem(a + e, na)
                for n in range(count):
                    block = full[n].at[pl.ds(slot(aa, zz, 0), ny)]
                    if e:
                        remote(block, block, s3.at[step, 0, 0, n], r3.at[zz, aa, 0, n], item, row).wait_recv()
                    remote(block, block, s4.at[e, step, n], r4.at[aa, zz, n], a * 2 + 1 - c, row).start()

        for t in range(nz + 2):
            if t < nz:
                second(t)
            if t == 0:
                for d in (1, -1, 2, -2):
                    halo(d, True)
            if 0 <= t - 1 < nz:
                third(t - 1)
            if 0 <= t - 2 < nz:
                fourth(t - 2)
        for n in range(count):
            for step in range(nz):
                for d in range(1, ny):
                    part = full[n].at[slot(a, z, y)]
                    remote(part, part, s2.at[step, d, n], r2.at[z, y, n], item, row).wait_send()
                for d in range(1, na):
                    part = full[n].at[pl.ds(slot(a, z, 0), ny)]
                    remote(part, part, s3.at[step, d, 0, n], r3.at[z, a, 0, n], item, row).wait_send()

    @pl.when(c == 1)
    def _():
        def second(step):
            zz = near(z, step, nz)
            for n in range(count):
                if step:
                    wait1(zz, n)
                for d in range(1, na):
                    src = full[n].at[slot(a, zz, y)] if step else mine[n]
                    remote(src, full[n].at[slot(a, zz, y)], s2.at[step, d, n], r2.at[zz, a, n], lax.rem(a + d, na) * 2 + c, row).start()

        def third(step):
            zz = near(z, step, nz)
            for e in range(na):
                aa = lax.rem(a + e, na)
                for n in range(count):
                    part = full[n].at[slot(aa, zz, y)]
                    if e:
                        remote(part, part, s2.at[step, 0, n], r2.at[zz, aa, n], item, row).wait_recv()
                    if e == 0 and step == 0:
                        locals_[n].wait()
                    for d in range(1, ny):
                        remote(part, part, s3.at[step, e, d, n], r3.at[zz, aa, y, n], item, z * ny + lax.rem(y + d, ny)).start()

        def fourth(step):
            zz = near(z, step, nz)
            for e in range(na):
                aa = lax.rem(a + e, na)
                for n in range(count):
                    for d in range(1, ny):
                        yy = lax.rem(y + d, ny)
                        part = full[n].at[slot(aa, zz, yy)]
                        remote(part, part, s3.at[step, e, 0, n], r3.at[zz, aa, yy, n], item, row).wait_recv()
                    block = full[n].at[pl.ds(slot(aa, zz, 0), ny)]
                    remote(block, block, s4.at[e, step, n], r4.at[aa, zz, n], a * 2 + 1 - c, row).start()

        for t in range(nz + 2):
            if t < nz:
                second(t)
            if t == 0:
                for d in (1, -1, 2, -2):
                    halo(d, True)
            if 0 <= t - 1 < nz:
                third(t - 1)
            if 0 <= t - 2 < nz:
                fourth(t - 2)
        for n in range(count):
            for step in range(nz):
                part = full[n].at[slot(a, z, y)]
                for d in range(1, na):
                    remote(part, part, s2.at[step, d, n], r2.at[z, a, n], item, row).wait_send()
                for e in range(na):
                    for d in range(1, ny):
                        remote(part, part, s3.at[step, e, d, n], r3.at[z, a, y, n], item, row).wait_send()

    other = 1 - 2 * c
    for n in range(count):
        for d in range(1, nz):
            remote(mine[n], full[n].at[slot(a, z, y)], s1.at[d, n], r1.at[z, n], item, row).wait_send()
        for e in range(na):
            for step in range(nz):
                mineb = full[n].at[pl.ds(slot(a, z, 0), ny)]
                remote(mineb, mineb, s4.at[e, step, n], r4.at[0, 0, n], item, row).wait_send()
                theirs = full[n].at[pl.ds((e * 2 + 1 - c) * rows + step * ny, ny)]
                remote(theirs, theirs, s4.at[e, step, n], r4.at[e, step, n], item, row).wait_recv()
    for d in (1, -1, 2, -2):
        halo(d, False)
    locals_[count].wait()


def gather_all(mesh_shape, tokens, shards):
    na = mesh_shape["items"] // 2
    nz, ny = split_rows(mesh_shape["rows"])
    ndev = mesh_shape["items"] * mesh_shape["rows"]
    count = len(shards)
    nm = max(na, ny)
    dma = pltpu.SemaphoreType.DMA
    out_shape = [jax.ShapeDtypeStruct((2 * REACH + 1,) + tokens.shape, tokens.dtype)] + [
        jax.ShapeDtypeStruct((ndev,) + s.shape, s.dtype) for s in shards
    ]
    return pl.pallas_call(
        functools.partial(gather_kernel, na, nz, ny, count),
        out_shape=out_shape,
        in_specs=[pl.BlockSpec(memory_space=pltpu.VMEM)] * (1 + count),
        out_specs=[pl.BlockSpec(memory_space=pl.ANY)] * (1 + count),
        scratch_shapes=[
            dma((2 * REACH + 1,)), dma((2 * REACH + 1,)), dma((count + 1,)),
            dma((nz, count)), dma((nz, count)),
            dma((nz, nm, count)), dma((nz, nm, count)),
            dma((nz, na, ny, count)), dma((nz, na, ny, count)),
            dma((na, nz, count)), dma((na, nz, count)),
        ],
        compiler_params=pltpu.CompilerParams(collective_id=1, has_side_effects=True),
        name="gather_weights",
    )(tokens, *shards)


def scatter_kernel(na, nz, ny, plan, *refs):
    inputs = max(p[0] for p in plan) + 1
    given = refs[:inputs]
    outs = refs[inputs : 2 * inputs]
    scratch = refs[2 * inputs :]
    groups = (len(scratch) - 9) // 5
    bufs = [scratch[5 * g : 5 * g + 5] for g in range(groups)]
    load_sem, s0, r0, s1, r1, s2, r2, s3, r3 = scratch[5 * groups :]
    a, c, z, y = place(nz, ny)
    rows = nz * ny
    row = z * ny + y
    item = a * 2 + c

    barrier = pltpu.get_barrier_semaphore()

    def greet(i_, r_):
        pl.semaphore_signal(barrier, inc=1, device_id=(i_, r_), device_id_type=MESH)

    def at_z(d):
        return lax.rem(z + d, nz) * ny + y

    def at_y(d):
        return z * ny + lax.rem(y + d, ny)

    def at_a(d):
        return lax.rem(a + d, na) * 2 + c

    for d in range(1, nz):
        greet(item, at_z(d))
    for d in range(1, ny):
        greet(item, at_y(d))
    for d in range(1, na):
        greet(at_a(d), row)
    greet(a * 2 + 1 - c, row)
    pl.semaphore_wait(barrier, nz + ny + na - 2)

    def remote(src, dst, send, recv, i_, r_):
        return pltpu.make_async_remote_copy(
            src_ref=src, dst_ref=dst, send_sem=send, recv_sem=recv, device_id=(i_, r_), device_id_type=MESH
        )

    order, seen = [], {}
    for p in plan:
        order.append(seen.get(p[3], 0))
        seen[p[3]] = order[-1] + 1

    def buf(k, which):
        return bufs[plan[k][3]][which].at[order[k]]

    def source(k, item_, zz):
        ref, (number, first, column, group) = given[plan[k][0]], plan[k]
        height, width = bufs[group][0].shape[-2:]
        return ref.at[pl.ds(item_ * rows + zz * ny, ny), pl.ds(first, height), pl.ds(column, width)]

    def load(k, aa, zz):
        return pltpu.make_async_copy(source(k, aa * 2 + c, zz), buf(k, 0).at[aa, zz], load_sem.at[k, aa, zz])

    def core(k, aa, zz):
        return remote(
            source(k, aa * 2 + 1 - c, zz), buf(k, 1).at[aa, zz], s0.at[k, aa, zz], r0.at[k, aa, zz], a * 2 + 1 - c, row
        )

    def first0(k, d, zz):
        aa = lax.rem(a + d, na)
        return remote(
            buf(k, 0).at[aa, zz], buf(k, 2).at[pl.ds((d - 1) * rows + zz * ny, ny)],
            s1.at[k, d, zz], r1.at[k, d, zz], at_a(d), row,
        )

    def first1(k, d, aa):
        return remote(
            buf(k, 0).at[aa, :, lax.rem(y + d, ny)], buf(k, 2).at[pl.ds((d - 1) * na * nz + aa * nz, nz)],
            s1.at[k, d, aa], r1.at[k, d, aa], item, at_y(d),
        )

    def second0(k, d):
        return remote(
            buf(k, 0).at[a, :, lax.rem(y + d, ny)], buf(k, 3).at[pl.ds((d - 1) * nz, nz)],
            s2.at[k, d], r2.at[k, d], item, at_y(d),
        )

    def second1(k, d):
        return remote(
            buf(k, 0).at[lax.rem(a + d, na), :, y], buf(k, 3).at[pl.ds((d - 1) * nz, nz)],
            s2.at[k, d], r2.at[k, d], at_a(d), row,
        )

    def third(k, d):
        return remote(
            buf(k, 0).at[a, lax.rem(z + d, nz), y], buf(k, 4).at[d - 1], s3.at[k, d], r3.at[k, d], item, at_z(d)
        )

    def summed(refs_):
        total = refs_[0][...].astype(jnp.float32)
        for ref in refs_[1:]:
            total = total + ref[...].astype(jnp.float32)
        return total

    def add_into(dst, parts):
        dst[...] = summed([dst] + parts).astype(dst.dtype)

    chunks = range(len(plan))
    for k in chunks:
        for e in range(na):
            for zz in range(nz):
                core(k, lax.rem(a + 1 + e, na), zz).start()
                load(k, lax.rem(a + 1 + e, na), zz).start()

    def stage1(k):
        for e in range(na):
            aa = lax.rem(a + 1 + e, na)
            for zz in range(nz):
                load(k, aa, zz).wait()
                core(k, aa, zz).wait_recv()

                @pl.loop(0, ny)
                def _(yy):
                    add_into(buf(k, 0).at[aa, zz, yy], [buf(k, 1).at[aa, zz, yy]])

                if e < na - 1:

                    @pl.when(c == 0)
                    def _():
                        first0(k, e + 1, zz).start()

        @pl.when(c == 1)
        def _():
            for d in range(1, ny):
                for aa in range(na):
                    first1(k, d, aa).start()

    def stage2(k):
        @pl.when(c == 0)
        def _():
            for zz in range(nz):
                for d in range(1, na):
                    first0(k, d, zz).wait_recv()

                @pl.loop(0, ny)
                def _(yy):
                    add_into(
                        buf(k, 0).at[a, zz, yy], [buf(k, 2).at[(d - 1) * rows + zz * ny + yy] for d in range(1, na)]
                    )

            for d in range(1, ny):
                second0(k, d).start()

        @pl.when(c == 1)
        def _():
            for e in range(na):
                for d in range(1, ny):
                    for aa in range(na):
                        if e == 0:
                            first1(k, d, aa).wait_recv()
                aa = lax.rem(a + 1 + e, na)

                @pl.loop(0, nz)
                def _(zz):
                    add_into(
                        buf(k, 0).at[aa, zz, y],
                        [buf(k, 2).at[(d - 1) * na * nz + aa * nz + zz] for d in range(1, ny)],
                    )

            for d in range(1, na):
                second1(k, d).start()

    def stage3(k):
        width = na if na > ny else ny
        for d in range(1, width):
            if d < ny and d < na:
                second0(k, d).wait_recv()
            elif d < ny:

                @pl.when(c == 0)
                def _():
                    second0(k, d).wait_recv()

            else:

                @pl.when(c == 1)
                def _():
                    second1(k, d).wait_recv()

        def add_second(peers):
            @pl.loop(0, nz)
            def _(zz):
                add_into(buf(k, 0).at[a, zz, y], [buf(k, 3).at[(d - 1) * nz + zz] for d in range(1, peers)])

        if na == ny:
            add_second(na)
        else:

            @pl.when(c == 0)
            def _():
                add_second(ny)

            @pl.when(c == 1)
            def _():
                add_second(na)

        for d in range(1, nz):
            third(k, d).start()

    def stage4(k):
        for d in range(1, nz):
            third(k, d).wait_recv()
        number, first, column, group = plan[k]
        height, width = bufs[group][0].shape[-2:]
        outs[number][first : first + height, column : column + width] = summed(
            [buf(k, 0).at[a, z, y]] + [buf(k, 4).at[d - 1] for d in range(1, nz)]
        )

    stages = (stage1, stage2, stage3, stage4)
    for t in range(len(plan) + 3):
        for n, stage in enumerate(stages):
            if 0 <= t - n < len(plan):
                stage(t - n)

    for k in chunks:
        for aa in range(na):
            for zz in range(nz):
                core(k, aa, zz).wait_send()
        for d in range(1, nz):
            third(k, d).wait_send()

        @pl.when(c == 0)
        def _():
            for d in range(1, na):
                for zz in range(nz):
                    first0(k, d, zz).wait_send()
            for d in range(1, ny):
                second0(k, d).wait_send()

        @pl.when(c == 1)
        def _():
            for d in range(1, ny):
                for aa in range(na):
                    first1(k, d, aa).wait_send()
            for d in range(1, na):
                second1(k, d).wait_send()


def scatter_all(mesh_shape, grads, pieces, collective_id=2):
    na = mesh_shape["items"] // 2
    nz, ny = split_rows(mesh_shape["rows"])
    plan, kinds, number = [], [], []
    for n, (g, (height, width)) in enumerate(zip(grads, pieces)):
        kind = (height, width, g.dtype)
        if kind not in kinds:
            kinds.append(kind)
            number.append(0)
        group = kinds.index(kind)
        for first in range(0, g.shape[1], height):
            for column in range(0, g.shape[2], width):
                plan.append((n, first, column, group))
                number[group] += 1
    scratch = []
    for (height, width, dtype), many in zip(kinds, number):
        one = (height, width)
        first = max((na - 1) * nz * ny, (ny - 1) * na * nz)
        second = (max(na, ny) - 1) * nz
        scratch += [
            pltpu.VMEM((many, na, nz, ny) + one, dtype),
            pltpu.VMEM((many, na, nz, ny) + one, dtype),
            pltpu.VMEM((many, first) + one, dtype),
            pltpu.VMEM((many, second) + one, dtype),
            pltpu.VMEM((many, nz - 1) + one, dtype),
        ]
    k = len(plan)
    dma = pltpu.SemaphoreType.DMA
    nm = max(na, ny)
    scratch += [dma((k, na, nz))] * 3 + [dma((k, nm, max(nz, na)))] * 2 + [dma((k, nm))] * 2 + [dma((k, nz))] * 2
    return pl.pallas_call(
        functools.partial(scatter_kernel, na, nz, ny, tuple(plan)),
        out_shape=[jax.ShapeDtypeStruct(g.shape[1:], jnp.float32) for g in grads],
        in_specs=[pl.BlockSpec(memory_space=pl.ANY)] * len(grads),
        out_specs=[pl.BlockSpec(memory_space=pltpu.VMEM)] * len(grads),
        scratch_shapes=scratch,
        compiler_params=pltpu.CompilerParams(
            collective_id=collective_id, has_side_effects=True, vmem_limit_bytes=60 << 20
        ),
        name="scatter_grads",
    )(*grads)


H = 12
HEAD = 64
PAIR = 2 * HEAD
MASKED = -1e30


def dot_last(x, y):
    return lax.dot_general(x, y, (((1,), (1,)), ((), ())), preferred_element_type=jnp.float32)


def dot_plain(x, y):
    return jnp.dot(x, y, preferred_element_type=jnp.float32)


def one_side(block, side, scale=1.0):
    lane = lax.broadcasted_iota(jnp.int32, (1, PAIR), 1)
    keep = (lane // HEAD == side).astype(jnp.float32) * scale
    return (block.astype(jnp.float32) * keep).astype(jnp.bfloat16)


def allowed_pairs(first, last, base, shape):
    place = lax.broadcasted_iota(jnp.int32, shape, 0)
    return (place >= first - base) & (place < last - base)


def skewed(count, *stages):
    held = [None] * count
    for t in range(count + len(stages) - 1):
        for k, stage in enumerate(stages):
            n = t - k
            if 0 <= n < count:
                held[n] = stage(n) if k == 0 else stage(n, held[n])
    return tuple(held)


def attend_kernel(tile, step, bounds, query, keys, values, first, last, low, full, logsum):
    pairs = query.shape[1] // PAIR
    for i in range(query.shape[0] // tile):
        rows = slice(i * tile, (i + 1) * tile)
        cols = [slice(p * PAIR, (p + 1) * PAIR) for p in range(pairs)]
        heads = [(c, s, one_side(query[rows, c], s, HEAD**-0.5)) for c in cols for s in range(2)]
        start_at, end_at = first[:, rows], last[:, rows]

        def body(j, carry):
            block = pl.ds(pl.multiple_of(j * step, step), step)
            allowed = allowed_pairs(start_at, end_at, j * step, (step, tile))
            turned = [values[block, c].T for c in cols]

            def score(n):
                c, s, q = heads[n]
                return jnp.where(allowed, dot_last(keys[block, c], q), MASKED)

            def soften(n, scores):
                top, total, acc = carry[n]
                peak = jnp.maximum(top, jnp.max(scores, axis=0, keepdims=True))
                lifted = jnp.exp(scores - peak)
                fade = jnp.exp(top - peak)
                return peak, total * fade + jnp.sum(lifted, axis=0, keepdims=True), fade, lifted.astype(jnp.bfloat16)

            def gather(n, soft):
                peak, total, fade, lifted = soft
                s = heads[n][1]
                return peak, total, carry[n][2] * fade + dot_plain(turned[n // 2][s * HEAD : (s + 1) * HEAD], lifted)

            return skewed(len(heads), score, soften, gather)

        start = tuple(
            (
                jnp.full((1, tile), MASKED, jnp.float32),
                jnp.zeros((1, tile), jnp.float32),
                jnp.zeros((HEAD, tile), jnp.float32),
            )
            for _ in heads
        )
        done = lax.fori_loop(bounds[0, i], bounds[1, i], body, start)
        for p, c in enumerate(cols):
            (top0, total0, acc0), (top1, total1, acc1) = done[2 * p : 2 * p + 2]
            result = jnp.concatenate([acc0 / total0, acc1 / total1], axis=0).T
            low[rows, c] = result.astype(jnp.bfloat16)
            full[rows, c] = result
            logsum[2 * p, :, rows] = top0 + jnp.log(total0)
            logsum[2 * p + 1, :, rows] = top1 + jnp.log(total1)


def columns(rows, group):
    return pl.BlockSpec((rows, group * HEAD), lambda p, b: (0, p))


def lines(length, group):
    return pl.BlockSpec((group, 1, length), lambda p, b: (p, 0, 0))


def whole(*shape):
    return pl.BlockSpec(shape, lambda p, b: (0,) * len(shape))


def cost(matmuls):
    return pl.CostEstimate(flops=matmuls * 2 * H * HEAD * 512 * 1536, bytes_accessed=12 << 20, transcendentals=0)


VMEM = pltpu.CompilerParams(vmem_limit_bytes=56 << 20)


def attend(bounds, query, keys, values, first, last, tile, step, group):
    tokens, width = query.shape
    wide = keys.shape[0]
    return pl.pallas_call(
        functools.partial(attend_kernel, tile, step),
        grid_spec=pltpu.PrefetchScalarGridSpec(
            num_scalar_prefetch=1,
            grid=(H // group,),
            in_specs=[columns(tokens, group), columns(wide, group), columns(wide, group)] + [whole(1, tokens)] * 2,
            out_specs=[columns(tokens, group), columns(tokens, group), lines(tokens, group)],
        ),
        out_shape=[
            jax.ShapeDtypeStruct((tokens, width), jnp.bfloat16),
            jax.ShapeDtypeStruct((tokens, width), jnp.float32),
            jax.ShapeDtypeStruct((H, 1, tokens), jnp.float32),
        ],
        compiler_params=VMEM,
        cost_estimate=cost(2),
        name="attend",
    )(bounds, query, keys, values, first, last)


def query_grad_kernel(tile, step, bounds, query, grad, keys, values, logsum, centre, first, last, out):
    pairs = query.shape[1] // PAIR
    for i in range(query.shape[0] // tile):
        rows = slice(i * tile, (i + 1) * tile)
        cols = [slice(p * PAIR, (p + 1) * PAIR) for p in range(pairs)]
        heads = [
            (
                c, s, one_side(query[rows, c], s, HEAD**-0.5), one_side(grad[rows, c], s),
                logsum[2 * p + s, :, rows], centre[2 * p + s, :, rows],
            )
            for p, c in enumerate(cols)
            for s in range(2)
        ]
        start_at, end_at = first[:, rows], last[:, rows]

        def body(j, carry):
            block = pl.ds(pl.multiple_of(j * step, step), step)
            allowed = allowed_pairs(start_at, end_at, j * step, (step, tile))
            turned = [keys[block, c].T for c in cols]

            def score(n):
                c, s, q, g, top, mid = heads[n]
                return dot_last(keys[block, c], q), dot_last(values[block, c], g)

            def soften(n, both):
                top, mid = heads[n][4:]
                weights = jnp.exp(jnp.where(allowed, both[0] - top, MASKED))
                return (weights * (both[1] - mid)).astype(jnp.bfloat16)

            def gather(n, d_scores):
                s = heads[n][1]
                return carry[n] + dot_plain(turned[n // 2][s * HEAD : (s + 1) * HEAD], d_scores)

            return skewed(len(heads), score, soften, gather)

        start = tuple(jnp.zeros((HEAD, tile), jnp.float32) for _ in heads)
        done = lax.fori_loop(bounds[0, i], bounds[1, i], body, start)
        for p, c in enumerate(cols):
            both = jnp.concatenate(done[2 * p : 2 * p + 2], axis=0) * HEAD**-0.5
            out[rows, c] = both.T.astype(jnp.bfloat16)


def query_grad(bounds, query, grad, keys, values, logsum, centre, first, last, tile, step, group):
    tokens, width = query.shape
    wide = keys.shape[0]
    return pl.pallas_call(
        functools.partial(query_grad_kernel, tile, step),
        grid_spec=pltpu.PrefetchScalarGridSpec(
            num_scalar_prefetch=1,
            grid=(H // group,),
            in_specs=[columns(tokens, group)] * 2
            + [columns(wide, group)] * 2
            + [lines(tokens, group)] * 2
            + [whole(1, tokens)] * 2,
            out_specs=columns(tokens, group),
        ),
        out_shape=jax.ShapeDtypeStruct((tokens, width), jnp.bfloat16),
        compiler_params=VMEM,
        cost_estimate=cost(3),
        name="query_grad",
    )(bounds, query, grad, keys, values, logsum, centre, first, last)


def key_grad_kernel(tile, step, start_row, bounds, keys, values, query, grad, logsum, centre, first, last, d_keys, d_values):
    pairs = keys.shape[1] // PAIR
    lane = lax.broadcasted_iota(jnp.int32, (1, PAIR), 1)
    for i in range(keys.shape[0] // tile):
        rows = slice(i * tile, (i + 1) * tile)
        cols = [slice(p * PAIR, (p + 1) * PAIR) for p in range(pairs)]
        heads = [
            (c, 2 * p + s, one_side(keys[rows, c], s, HEAD**-0.5), one_side(values[rows, c], s))
            for p, c in enumerate(cols)
            for s in range(2)
        ]

        def body(j, carry):
            block = pl.ds(pl.multiple_of(j * step, step), step)
            allowed = allowed_pairs(first[:, block], last[:, block], start_row + i * tile, (tile, step))

            def score(m):
                c, n, k, v = heads[m]
                return dot_last(k, query[block, c]), dot_last(v, grad[block, c])

            def soften(m, both):
                n = heads[m][1]
                weights = jnp.exp(jnp.where(allowed, both[0] - logsum[n, :, block], MASKED))
                return (weights * (both[1] - centre[n, :, block])).astype(jnp.bfloat16), weights.astype(jnp.bfloat16)

            def gather(m, soft):
                c = heads[m][0]
                return (
                    carry[m][0] + dot_plain(soft[0], query[block, c]),
                    carry[m][1] + dot_plain(soft[1], grad[block, c]),
                )

            return skewed(len(heads), score, soften, gather)

        zero = jnp.zeros((tile, PAIR), jnp.float32)
        done = lax.fori_loop(bounds[0, i], bounds[1, i], body, tuple((zero, zero) for _ in heads))
        for p, c in enumerate(cols):
            (k0, v0), (k1, v1) = done[2 * p : 2 * p + 2]
            d_keys[rows, c] = (jnp.where(lane < HEAD, k0, k1) * HEAD**-0.5).astype(jnp.bfloat16)
            d_values[rows, c] = jnp.where(lane < HEAD, v0, v1).astype(jnp.bfloat16)


def key_grad(bounds, keys, values, query, grad, logsum, centre, first, last, tile, step, group):
    tokens, width = keys.shape
    wide = query.shape[0]
    return pl.pallas_call(
        functools.partial(key_grad_kernel, tile, step, REACH * tokens),
        grid_spec=pltpu.PrefetchScalarGridSpec(
            num_scalar_prefetch=1,
            grid=(H // group,),
            in_specs=[columns(tokens, group)] * 2
            + [columns(wide, group)] * 2
            + [lines(wide, group)] * 2
            + [whole(1, wide)] * 2,
            out_specs=[columns(tokens, group), columns(tokens, group)],
        ),
        out_shape=[jax.ShapeDtypeStruct((tokens, width), jnp.bfloat16)] * 2,
        compiler_params=VMEM,
        cost_estimate=cost(4),
        name="key_grad",
    )(bounds, keys, values, query, grad, logsum, centre, first, last)


eps_norm = 1e-06
AXES = ("items", "rows")


NAMES = (
    "query_proj", "key_proj", "value_proj", "query_bias", "value_bias", "output_proj", "output_bias", "attn_gain",
    "attn_shift", "hidden_proj", "hidden_bias", "return_proj", "return_bias", "final_gain", "final_shift",
)


def dot_rows(matrix, factor):
    return lax.dot_general(matrix, factor, (((0,), (0,)), ((), ())), preferred_element_type=jnp.float32)


def layer_norm(hidden, norm_gain, norm_shift):
    row_mean = jnp.mean(hidden, axis=1, keepdims=True)
    centred = hidden - row_mean
    row_var = jnp.mean(centred * centred, axis=1, keepdims=True)
    return centred * lax.rsqrt(row_var + eps_norm) * norm_gain + norm_shift


def shifted(value, by):
    peers = lax.axis_size("rows")
    pairs = [(i, i + by) for i in range(peers) if 0 <= i + by < peers]
    return lax.ppermute(value, "rows", pairs)


def halo(value):
    return [value if d == 0 else shifted(value, -d) for d in range(-REACH, REACH + 1)]


def item_tables(lengths, position, rows_dev, tile, step):
    ends = jnp.cumsum(lengths, dtype=jnp.int32)
    wide = (2 * REACH + 1) * rows_dev
    base = position - REACH * rows_dev

    def item_of(places):
        low = jnp.max(jnp.where(ends[None, :] <= places[:, None], ends[None, :], 0), axis=1)
        high = jnp.min(jnp.where(ends[None, :] > places[:, None], ends[None, :], ends[-1]), axis=1)
        return low - base, high - base

    places = base + jnp.arange(wide, dtype=jnp.int32)
    first, last = item_of(places)
    inside = (places >= 0) & (places < ends[-1])
    first, last = jnp.where(inside, first, wide), jnp.where(inside, last, -1)
    starts = position + jnp.arange(0, rows_dev, tile, dtype=jnp.int32)
    bounds = jnp.stack([item_of(starts)[0] // step, (item_of(starts + tile - 1)[1] + step - 1) // step])
    return first[None, :], last[None, :], jnp.clip(bounds, 0, wide // step).astype(jnp.int32)


TILE, STEP, GROUP = 256, 256, 12


def per_device(mesh_shape, tokens, *given):
    names = NAMES
    part = dict(zip(names, given[:15]))
    item_lengths, out_grad = given[15:]
    matrices = ["query_proj", "key_proj", "value_proj", "output_proj", "hidden_proj", "return_proj"]
    vectors = [n for n in names if n not in matrices]
    ndev = mesh_shape["items"] * mesh_shape["rows"]
    rows_dev, width = tokens.shape
    aligned = all(part[n].shape[0] % 8 == 0 for n in matrices)
    sizes = [part[n].shape[0] for n in vectors]
    used = sum(sizes)
    padded = -(-used // 1024) * 1024
    packed = jnp.pad(jnp.concatenate([part[n] for n in vectors]), (0, padded - used)).reshape(8, padded // 8)
    if aligned:
        got = gather_all(mesh_shape, tokens, [part[n] for n in matrices] + [packed])
        window = got[0].reshape(-1, width)
        wholes = [g.reshape((-1,) + g.shape[2:]) for g in got[1:-1]]
        flat = got[-1]
    else:
        window = jnp.concatenate(halo(tokens))
        wholes = [lax.all_gather(part[n], AXES, axis=0, tiled=True) for n in matrices]
        flat = lax.all_gather(packed, AXES, axis=0, tiled=False)
    flat = flat.reshape(ndev, padded)
    W = dict(zip(matrices, wholes))
    at = 0
    for n, size in zip(vectors, sizes):
        W[n] = flat[:, at : at + size].reshape(-1).astype(jnp.float32)
        at += size

    position = lax.axis_index("rows") * rows_dev
    first, last, bounds = item_tables(item_lengths[0], position, rows_dev, TILE, STEP)
    own = slice(REACH * rows_dev, (REACH + 1) * rows_dev)
    own_items = first[:, own], last[:, own]

    query_wide = (dot_plain(window, W["query_proj"]) + W["query_bias"]).astype(jnp.bfloat16)
    keys_wide = dot_plain(window, W["key_proj"]).astype(jnp.bfloat16)
    values_wide = (dot_plain(window, W["value_proj"]) + W["value_bias"]).astype(jnp.bfloat16)
    query, keys, values = query_wide[own], keys_wide[own], values_wide[own]
    attended, attended_full, logsum = attend(
        bounds, query, keys_wide, values_wide, *own_items, TILE, STEP, GROUP
    )

    mixed = tokens.astype(jnp.float32) + (dot_plain(attended, W["output_proj"]) + W["output_bias"])
    normed, attn_back = jax.vjp(layer_norm, mixed, W["attn_gain"], W["attn_shift"])
    normed_low = normed.astype(jnp.bfloat16)
    hidden_pre = dot_plain(normed_low, W["hidden_proj"]) + W["hidden_bias"]
    cdf = 0.5 * (1.0 + lax.erf(hidden_pre * (0.5**0.5)))
    active = (hidden_pre * cdf).astype(jnp.bfloat16)
    slope = cdf + hidden_pre * jnp.exp(-0.5 * hidden_pre * hidden_pre) * 0.3989422804014327
    second = normed + (dot_plain(active, W["return_proj"]) + W["return_bias"])
    result, final_back = jax.vjp(layer_norm, second, W["final_gain"], W["final_shift"])

    grads = {}
    d_second, grads["final_gain"], grads["final_shift"] = final_back(out_grad.astype(jnp.float32))
    d_ffn = d_second.astype(jnp.bfloat16)
    grads["return_bias"] = jnp.sum(d_ffn.astype(jnp.float32), axis=0)
    d_hidden = (dot_last(d_ffn, W["return_proj"]) * slope).astype(jnp.bfloat16)
    grads["hidden_bias"] = jnp.sum(d_hidden.astype(jnp.float32), axis=0)
    d_normed = dot_last(d_hidden, W["hidden_proj"]) + d_second
    d_mixed, grads["attn_gain"], grads["attn_shift"] = attn_back(d_normed)
    d_branch = d_mixed.astype(jnp.bfloat16)
    grads["output_bias"] = jnp.sum(d_branch.astype(jnp.float32), axis=0)
    d_attended = dot_last(d_branch, W["output_proj"]).astype(jnp.bfloat16)

    lanes = jnp.arange(width, dtype=jnp.int32)[None, :] // HEAD == jnp.arange(16, dtype=jnp.int32)[:, None]
    centre = lax.dot_general(
        lanes.astype(jnp.float32), d_attended.astype(jnp.float32) * attended_full, (((1,), (1,)), ((), ())),
        precision=lax.Precision.HIGHEST,
    )[:H, None]
    stats = jnp.concatenate([logsum, centre])
    grad_wide = jnp.concatenate(halo(d_attended))
    stats_wide = jnp.concatenate(halo(stats), axis=2)
    grads["return_proj"] = dot_rows(active, d_ffn)
    grads["hidden_proj"] = dot_rows(normed_low, d_hidden)
    grads["output_proj"] = dot_rows(attended, d_branch)
    d_query = query_grad(
        bounds, query, d_attended, keys_wide, values_wide, logsum, centre, *own_items, TILE, STEP, GROUP
    )
    d_keys, d_values = key_grad(
        bounds, keys, values, query_wide, grad_wide, stats_wide[:H], stats_wide[H:], first, last, TILE, STEP, GROUP
    )
    grads["query_proj"] = dot_rows(tokens, d_query)
    grads["key_proj"] = dot_rows(tokens, d_keys)
    grads["value_proj"] = dot_rows(tokens, d_values)
    grads["query_bias"] = jnp.sum(d_query.astype(jnp.float32), axis=0)
    grads["value_bias"] = jnp.sum(d_values.astype(jnp.float32), axis=0)
    tokens_grad = (
        d_mixed
        + dot_last(d_query, W["query_proj"])
        + dot_last(d_keys, W["key_proj"])
        + dot_last(d_values, W["value_proj"])
    )

    rows_of = jnp.concatenate([grads[n].reshape(ndev, size) for n, size in zip(vectors, sizes)], axis=1)
    rows_of = jnp.pad(rows_of, ((0, 0), (0, padded - used))).reshape(ndev, 8, padded // 8)
    low = [grads[n].astype(jnp.bfloat16).reshape((ndev, -1) + grads[n].shape[1:]) for n in matrices]
    if aligned:
        height = min(g.shape[1] for g in low)
        sums = scatter_all(mesh_shape, low + [rows_of], [(height, width)] * len(low) + [rows_of.shape[1:]])
    else:
        sums = [lax.psum_scatter(g, AXES, scatter_dimension=0, tiled=True)[0] for g in low + [rows_of]]
    total = {n: s.astype(jnp.float32) for n, s in zip(matrices, sums)}
    line = sums[-1].reshape(padded)
    at = 0
    for n, size in zip(vectors, sizes):
        total[n] = line[at : at + size]
        at += size
    return (result.astype(jnp.bfloat16), tokens_grad) + tuple(total[n] for n in names)


def solution(mesh):
    both = P(AXES)
    return jax.shard_map(
        functools.partial(per_device, dict(mesh.shape)),
        mesh=mesh,
        in_specs=(both,) * 16 + (P("items"), both),
        out_specs=(both,) * 17,
        check_vma=False,
    )
```

time: 1480 us -> 445 us (0.30)
  waiting for transfers between devices: 744 us -> 25.4 us
  matrix products: 385 us -> 72.6 us
  Pallas kernels: 0 us -> 263 us
  blocking collectives: 118 us -> 0 us
  local copies, waits for them, and re-layouts: 121 us -> 31.9 us
  other arithmetic: 49.4 us -> 11.4 us
    reduce_scatter x3 -> x0, waiting for transfers between devices: 283 us -> none  [the longest x1 142 us: per_device(): lax.psum_scatter(grad_return_proj, ('items', 'rows'), scatter_dimension=0...]
    pallas_call x0 -> x5, Pallas kernels: none -> 263 us  [the longest x1 99 us: scatter_all(): pl.pallas_call(functools.partial(scatter_kernel, na, nz, ny, tuple(plan))...]
    dot_general x101 -> x13, matrix products: 302 us -> 52.5 us  [the longest x6 32.7 us: dot_plain(): return jnp.dot(x, y, preferred_element_type=jnp.float32)]
    all_gather x6 -> x0, waiting for transfers between devices: 225 us -> none  [the longest x1 74.1 us: per_device(): lax.all_gather(query_proj, ('items', 'rows'), axis=0, tiled=True)]
    unnamed x15 -> x0, waiting for transfers between devices: 135 us -> none
    unnamed x2 -> x0, blocking collectives: 118 us -> none
    ppermute x12 -> x8, waiting for transfers between devices: 101 us -> 25.4 us  [shifted(): return lax.ppermute(value, 'rows', pairs)]
    dot_general x30 -> x6, matrix products: 82.9 us -> 20.1 us  [dot_rows(): lax.dot_general(matrix, factor, (((0,), (0,)), ((), ())), preferred_eleme...]
  transfers between devices with their start and end apart: 24 -> 8, of which waited for: 15 -> 2; matrix products, arithmetic and copies ran while one was open for 23% -> 6% of each run, Pallas kernels for 0% -> 4%
where the time goes in v1:
time: 445 us; the launch traced here: 443 us
  Pallas kernels  263 us (59%)
  matrix products  72.6 us (16%)
  starting transfers between devices  37.6 us (8%)
  local copies, waits for them, and re-layouts  31.9 us (7%)
  waiting for transfers between devices  25.4 us (6%)
  other arithmetic  11.4 us (3%)
    pallas_call x1, Pallas kernels, scatter_all(): pl.pallas_call(functools.partial(scatter_kernel, na, nz, ny, tuple(plan))...  99 us
    pallas_call x1, Pallas kernels, gather_all(): pl.pallas_call(functools.partial(gather_kernel, na, nz, ny, count), out_s...  97.5 us
    ppermute x8, starting transfers between devices, shifted(): return lax.ppermute(value, 'rows', pairs)  37.6 us
    dot_general x6, matrix products, dot_plain(): return jnp.dot(x, y, preferred_element_type=jnp.float32)  32.7 us
    pallas_call x1, Pallas kernels, key_grad(): pl.pallas_call(functools.partial(key_grad_kernel, tile, step, REACH * tok...  26.1 us
    ppermute x8, waiting for transfers between devices, shifted(): return lax.ppermute(value, 'rows', pairs)  25.4 us
    pallas_call x1, Pallas kernels, attend(): pl.pallas_call(functools.partial(attend_kernel, tile, step), grid_spec=pl...  21.9 us
    dot_general x6, matrix products, dot_rows(): lax.dot_general(matrix, factor, (((0,), (0,)), ((), ())), preferred_eleme...  20.1 us
  transfers between devices with their start and end apart: 8, of which 2 were waited for; matrix products, arithmetic and copies ran while one was open for 6% of the time, Pallas kernels for 4%

profile of v1, /device:TPU:0, one launch (start us, length us, event | category | flops | bytes accessed | tf_op | source)
XLA Modules:
  0.0 443.3 jit_solution(9129408343788569431)
XLA Ops:
  0.7 6.1 %concatenate.15 = bf16[288]{0:T(512)(128)(2,1)S(1)} concatenate(bf16[24]{0:T(256)(128)(2,1)} %param.22, bf16[24]{0:T(256)(128)(2,1)} %param.23, bf16[24]{0:T(256)(128)(2,1)} %param.25, bf16[24]{0:T(256)(128)(2,1)} %param.26, bf16[24]{0:T(256)(128)(2,1)} %param.27, bf16[96]{0:T(256)(128)(2,1)} %param.29, bf16[24]{0:T(256)(128)(2,1)} %param.31, bf16[24]{0:T(256)(128)(2,1)} %param.32, ...), dimensions={0} | concatenate | bytes 1152 | tf_op jit(solution)/shard_map/concatenate | solution.py:855
  7.4 97.5 %gather_weights.1 = (bf16[5,512,768]{2,1,0:T(8,128)(2,1)}, bf16[32,24,768]{2,1,0:T(8,128)(2,1)}, bf16[32,24,768]{2,1,0:T(8,128)(2,1)}, bf16[32,24,768]{2,1,0:T(8...) custom-call(bf16[512,768]{1,0:T(8,128)(2,1)} %refs_0_.1, ...), custom_call_target="tpu_custom_call" | custom-call | tf_op jit(solution)/shard_map/gather_weights/pallas_call | solution.py:237
  109.6 5.8 %add_convert_fusion.1.query = bf16[2560,768]{1,0:T(8,128)(2,1)S(1)} fusion(bf16[2560,768]{1,0:T(8,128)(2,1)} %bitcast.104, bf16[768,768]{1,0:T(8,128)(2,1)} %bitcast.109, f32[768]{0:T(1024)S(1)} %reshape.487), kind=kOutput, calls=%fused_computation.2 | convolution fusion | flops 3023831040 | bytes 9047040 | tf_op jit(solution)/shard_map/dot_general | solution.py:550
  117.6 4.8 %convolution_convert_fusion.keys = bf16[2560,768]{1,0:T(8,128)(2,1)} fusion(bf16[2560,768]{1,0:T(8,128)(2,1)S(1)} %bitcast.106, bf16[768,768]{1,0:T(8,128)(2,1)S(1)} %bitcast.108), kind=kOutput, calls=%fused_computation.12 | convolution fusion | flops 3021864960 | bytes 9043968 | tf_op jit(solution)/shard_map/dot_general | solution.py:550
  122.5 7.3 %add_convert_fusion.values = bf16[2560,768]{1,0:T(8,128)(2,1)} fusion(bf16[2560,768]{1,0:T(8,128)(2,1)} %bitcast.105, bf16[768,768]{1,0:T(8,128)(2,1)S(1)} %bitcast.84, f32[768]{0:T(1024)S(1)} %reshape.488), kind=kOutput, calls=%fused_computation.1 | convolution fusion | flops 3023831040 | bytes 9047040 | tf_op jit(solution)/shard_map/dot_general | solution.py:550
  130.4 21.9 %attend.1 = (bf16[512,768]{1,0:T(8,128)(2,1)}, f32[512,768]{1,0:T(8,128)}, f32[12,1,512]{2,1,0:T(1,128)}) custom-call(s32[2,2]{1,0:T(2,128)} %add_clamp_fusion.bounds, bf16[512,768]{1,0:T(8,128)(2,1)} %slice.113.query, bf16[2560,768]{1,0:T(8,128)(2,1)} %convolution_convert_fusion.keys, bf16[2560,768]{1,0:T(8,128)(2,1)} %add_convert_fusion.values, ...), custom_call_target="tpu_custom_call" | custom-call | flops 2415919104 | bytes 12582912 | tf_op jit(solution)/shard_map/attend/pallas_call | solution.py:645
  154.9 6.6 %multiply_convert_fusion = (bf16[512,3072]{1,0:T(8,128)(2,1)S(1)}, f32[512,3072]{1,0:T(8,128)}) fusion(f32[3072]{0:T(1024)S(1)} %reshape.492, bf16[768,3072]{1,0:T(8,128)(2,1)} %bitcast.98, f32[512,768]{1,0:T(8,128)S(1)} %get-tuple-element.95, f32[768]{0:T(1024)S(1)} %reshape.491, f32[768]{0:T(1024)S(1)} %reshape.490, f32[512]{0:T(512)S(1)} %fusion.19, ...), kind=kOutput, calls=%fused_computation.10 | convolution fusion | flops 2427322368 | bytes 15751168 | tf_op jit(solution)/shard_map/dot_general | solution.py:550
  161.6 6.2 %fusion.31 = (f32[512]{0:T(512)S(1)}, f32[512,768]{1,0:T(8,128)S(1)}) fusion(f32[768]{0:T(1024)S(1)} %reshape.493, bf16[512,3072]{1,0:T(8,128)(2,1)S(1)} %get-tuple-element.96, bf16[3072,768]{1,0:T(8,128)(2,1)} %bitcast.102, f32[768]{0:T(1024)S(1)} %reshape.491, f32[768]{0:T(1024)S(1)} %reshape.490, f32[512]{0:T(512)S(1)} %fusion.19, ...), kind=kOutput, calls=%fused_computation.125 | convolution fusion | flops 2418671104 | bytes 11025408 | tf_op jit(solution)/shard_map/dot_general | solution.py:550
  170.1 2.9 fusion.27
  173.2 6.6 %convert_reduce_fusion = (f32[3072]{0:T(1024)S(1)}, bf16[512,3072]{1,0:T(8,128)(2,1)S(1)}) fusion(f32[512,3072]{1,0:T(8,128)S(1)} %copy-done.28, f32[3072]{0:T(1024)S(1)} %reshape.492, bf16[512,768]{1,0:T(8,128)(2,1)S(1)} %get-tuple-element.68, bf16[3072,768]{1,0:T(8,128)(2,1)} %bitcast.103), kind=kOutput, calls=%fused_computation.9 | convolution fusion | flops 2436363264 | bytes 14966784 | tf_op jit(solution)/shard_map/dot_general | solution.py:546
  179.8 3.2 multiply_reduce_fusion
  189.9 15.8 %collective-permute-start.4 = (f32[24,1,512]{2,1,0:T(1,128)}, f32[24,1,512]{2,1,0:T(1,128)S(1)}, u32[]{:S(2)}, u32[]{:S(2)}) collective-permute-start(f32[24,1,512]{2,1,0:T(1,128)} %constant_dynamic-update-slice_fusion.5), channel_id=1, source_target_pairs={{0,2},{1,3},{2,4},{3,5},{4,6},{5,7},{8,10},{9,11},{10,12},{11,13},... | collective-permute-start | bytes 147464 | tf_op jit(solution)/shard_map/ppermute | solution.py:814
  209.6 10.0 %collective-permute-start = (bf16[512,768]{1,0:T(8,128)(2,1)}, bf16[512,768]{1,0:T(8,128)(2,1)}, u32[]{:S(2)}, u32[]{:S(2)}) collective-permute-start(bf16[512,768]{1,0:T(8,128)(2,1)} %convolution_convert_fusion.7.grad), channel_id=1, source_target_pairs={{0,2},{1,3},{2,4},{3,5},{4,6},{5,7},{8,10},{9,11},{10,12},{11,13},... | collective-permute-start | bytes 2359304 | tf_op jit(solution)/shard_map/ppermute | solution.py:814
  220.3 4.8 %convolution_convert_fusion.2 = bf16[768,3072]{1,0:T(8,128)(2,1)} fusion(bf16[512,3072]{1,0:T(8,128)(2,1)S(1)} %get-tuple-element.102, f32[512,768]{1,0:T(8,128)S(1)} %get-tuple-element.95, f32[768]{0:T(1024)S(1)} %reshape.491, f32[768]{0:T(1024)S(1)} %reshape.490, f32[512]{0:T(512)S(1)} %fusion.19, f32[512]{0:T(512)S(1)} %broadcast_multiply_fusion.1), kind=kOutput, calls=%fused_computation.14 | convolution fusion | flops 2420244480 | bytes 9447424 | tf_op jit(solution)/shard_map/dot_general | solution.py:801
  225.1 4.4 convolution_convert_fusion.1
  231.3 18.4 %query_grad.1 = bf16[512,768]{1,0:T(8,128)(2,1)} custom-call(s32[2,2]{1,0:T(2,128)} %add_clamp_fusion.bounds, bf16[512,768]{1,0:T(8,128)(2,1)} %slice.113.query, bf16[512,768]{1,0:T(8,128)(2,1)} %convolution_convert_fusion.7.grad, bf16[2560,768]{1,0:T(8,128)(2,1)} %convolution_convert_fusion.keys, bf16[2560,768]{1,0:T(8,128)(2,1)} %add_convert_fusion.values, ...), custom_call_target="tpu_custom_call" | custom-call | flops 3623878656 | bytes 12582912 | tf_op jit(solution)/shard_map/query_grad/pallas_call | solution.py:709
  249.7 3.1 convolution_convert_fusion.6
  259.8 5.3 %collective-permute-start.1 = (bf16[512,768]{1,0:T(8,128)(2,1)}, bf16[512,768]{1,0:T(8,128)(2,1)S(1)}, u32[]{:S(2)}, u32[]{:S(2)}) collective-permute-start(bf16[512,768]{1,0:T(8,128)(2,1)} %convolution_convert_fusion.7.grad), channel_id=1, source_target_pairs={{0,1},{1,2},{2,3},{3,4},{4,5},{5,6},{6,7},{8,9},{9,10},{10,11},{11... | collective-permute-start | bytes 2359304 | tf_op jit(solution)/shard_map/ppermute | solution.py:814
  269.8 22.1 %collective-permute-done.1 = bf16[512,768]{1,0:T(8,128)(2,1)S(1)} collective-permute-done((bf16[512,768]{1,0:T(8,128)(2,1)}, bf16[512,768]{1,0:T(8,128)(2,1)S(1)}, u32[]{:S(2)}, u32[]{:S(2)}) %collective-permute-start.1) | collective-permute-done | bytes 786464 | tf_op jit(solution)/shard_map/ppermute | solution.py:814
  293.2 3.3 collective-permute-done.3
  298.5 26.1 %key_grad.1 = (bf16[512,768]{1,0:T(8,128)(2,1)}, bf16[512,768]{1,0:T(8,128)(2,1)}) custom-call(s32[2,2]{1,0:T(2,128)} %add_clamp_fusion.bounds, bf16[512,768]{1,0:T(8,128)(2,1)} %slice.124.keys, bf16[512,768]{1,0:T(8,128)(2,1)} %slice.125.values, bf16[2560,768]{1,0:T(8,128)(2,1)} %copy-done.10, bf16[2560,768]{1,0:T(8,128)(2,1)} %copy-done.11, ...), custom_call_target="tpu_custom_call" | custom-call | flops 4831838208 | bytes 12582912 | tf_op jit(solution)/shard_map/key_grad/pallas_call | solution.py:772
  325.9 3.0 convolution_convert_fusion.4
  329.8 3.0 convolution_convert_fusion.5
  332.8 99.0 %scatter_grads.1 = (f32[24,768]{1,0:T(8,128)}, f32[24,768]{1,0:T(8,128)}, f32[24,768]{1,0:T(8,128)}, f32[24,768]{1,0:T(8,128)}, f32[24,3072]{1,0:T(8,128)}, /*index=5*/f32[96,768]{1,0:T(8,128)}, f32[8,128]{1,0:T(8,128)}) custom-call(bf16[32,24,768]{2,1,0:T(8,128)(2,1)} %bitcast.87, bf16[32,24,768]{2,1,0:T(8,128)(2,1)} %bitcast.89, ...), custom_call_target="tpu_custom_call" | custom-call | tf_op jit(solution)/shard_map/scatter_grads/pallas_call | solution.py:526
  (167 shorter events, 54.6 us)
Async XLA Ops:
  0.7 105.3 %copy-start.25 = (s32[1,8]{1,0:T(1,128)S(1)}, s32[1,8]{1,0:T(1,128)}, u32[]{:S(2)}) copy-start(s32[1,8]{1,0:T(1,128)} %param.34) | copy-start | bytes 100
  108.2 7.2 %copy-start.18 = (s32[1,2560]{1,0:T(1,128)}, s32[1,2560]{1,0:T(1,128)S(1)}, u32[]{:S(2)}) copy-start(s32[1,2560]{1,0:T(1,128)S(1)} %get-tuple-element.105.last) | copy-start | bytes 30724
  108.2 7.2 %copy-start.19 = (s32[1,2560]{1,0:T(1,128)}, s32[1,2560]{1,0:T(1,128)S(1)}, u32[]{:S(2)}) copy-start(s32[1,2560]{1,0:T(1,128)S(1)} %get-tuple-element.106.first) | copy-start | bytes 30724
  109.6 8.0 %copy-start.20 = (bf16[5,512,768]{2,1,0:T(8,128)(2,1)S(1)}, bf16[5,512,768]{2,1,0:T(8,128)(2,1)}, u32[]{:S(2)}) copy-start(bf16[5,512,768]{2,1,0:T(8,128)(2,1)} %get-tuple-element.37) | copy-start | bytes 11796484
  115.4 6.9 %copy-start.10 = (bf16[2560,768]{1,0:T(8,128)(2,1)}, bf16[2560,768]{1,0:T(8,128)(2,1)S(1)}, u32[]{:S(2)}) copy-start(bf16[2560,768]{1,0:T(8,128)(2,1)S(1)} %add_convert_fusion.1.query) | copy-start | bytes 11796484
  117.6 4.9 %copy-start.3 = (bf16[32,24,768]{2,1,0:T(8,128)(2,1)S(1)}, bf16[32,24,768]{2,1,0:T(8,128)(2,1)}, u32[]{:S(2)}) copy-start(bf16[32,24,768]{2,1,0:T(8,128)(2,1)} %get-tuple-element.41) | copy-start | bytes 3538948
  130.4 21.9 %copy-start.5 = (bf16[512,768]{1,0:T(8,128)(2,1)S(1)}, bf16[512,768]{1,0:T(8,128)(2,1)}, u32[]{:S(2)}) copy-start(bf16[512,768]{1,0:T(8,128)(2,1)} %refs_0_.1) | copy-start | bytes 2359300
  130.4 21.9 %copy-start.23 = (bf16[32,24,768]{2,1,0:T(8,128)(2,1)S(1)}, bf16[32,24,768]{2,1,0:T(8,128)(2,1)}, u32[]{:S(2)}) copy-start(bf16[32,24,768]{2,1,0:T(8,128)(2,1)} %get-tuple-element.43) | copy-start | bytes 3538948
  161.6 6.2 %copy-start.29 = (bf16[512,3072]{1,0:T(8,128)(2,1)}, bf16[512,3072]{1,0:T(8,128)(2,1)S(1)}, u32[]{:S(2)}) copy-start(bf16[512,3072]{1,0:T(8,128)(2,1)S(1)} %get-tuple-element.96) | copy-start | bytes 9437188
  173.0 6.8 %slice-start = ((s8[4718592]{0:T(1024)(128)(4,1)}), s8[4194304]{0:T(1024)(128)(4,1)S(1)}, s32[]{:S(2)}) async-start(s8[4718592]{0:T(1024)(128)(4,1)} %bitcast.99), calls=%async_computation | async-start | bytes 8388608
  173.2 6.6 %slice-start.1 = ((s8[4718592]{0:T(1024)(128)(4,1)}), s8[524288]{0:T(1024)(128)(4,1)S(1)}, s32[]{:S(2)}) async-start(s8[4718592]{0:T(1024)(128)(4,1)} %bitcast.99), calls=%async_computation.1 | async-start | bytes 1048576
  189.9 69.8 %collective-permute-start.4 = (f32[24,1,512]{2,1,0:T(1,128)}, f32[24,1,512]{2,1,0:T(1,128)S(1)}, u32[]{:S(2)}, u32[]{:S(2)}) collective-permute-start(f32[24,1,512]{2,1,0:T(1,128)} %constant_dynamic-update-slice_fusion.5), channel_id=1, source_target_pairs={{0,2},{1,3},{2,4},{3,5},{4,6},{5,7},{8,10},{9,11},{10,12},{11,13},... | collective-permute-start | bytes 147464 | tf_op jit(solution)/shard_map/ppermute | solution.py:814
  205.7 59.4 %collective-permute-start.5 = (f32[24,1,512]{2,1,0:T(1,128)}, f32[24,1,512]{2,1,0:T(1,128)S(1)}, u32[]{:S(2)}, u32[]{:S(2)}) collective-permute-start(f32[24,1,512]{2,1,0:T(1,128)} %constant_dynamic-update-slice_fusion.5), channel_id=1, source_target_pairs={{0,1},{1,2},{2,3},{3,4},{4,5},{5,6},{6,7},{8,9},{9,10},{10,11},{11... | collective-permute-start | bytes 147464 | tf_op jit(solution)/shard_map/ppermute | solution.py:814
  207.0 59.5 %collective-permute-start.6 = (f32[24,1,512]{2,1,0:T(1,128)}, f32[24,1,512]{2,1,0:T(1,128)S(1)}, u32[]{:S(2)}, u32[]{:S(2)}) collective-permute-start(f32[24,1,512]{2,1,0:T(1,128)} %constant_dynamic-update-slice_fusion.5), channel_id=1, source_target_pairs={{1,0},{2,1},{3,2},{4,3},{5,4},{6,5},{7,6},{9,8},{10,9},{11,10},{12... | collective-permute-start | bytes 147464 | tf_op jit(solution)/shard_map/ppermute | solution.py:814
  208.3 59.5 %collective-permute-start.7 = (f32[24,1,512]{2,1,0:T(1,128)}, f32[24,1,512]{2,1,0:T(1,128)S(1)}, u32[]{:S(2)}, u32[]{:S(2)}) collective-permute-start(f32[24,1,512]{2,1,0:T(1,128)} %constant_dynamic-update-slice_fusion.5), channel_id=1, source_target_pairs={{2,0},{3,1},{4,2},{5,3},{6,4},{7,5},{10,8},{11,9},{12,10},{13,11},... | collective-permute-start | bytes 147464 | tf_op jit(solution)/shard_map/ppermute | solution.py:814
  209.6 59.0 %collective-permute-start = (bf16[512,768]{1,0:T(8,128)(2,1)}, bf16[512,768]{1,0:T(8,128)(2,1)}, u32[]{:S(2)}, u32[]{:S(2)}) collective-permute-start(bf16[512,768]{1,0:T(8,128)(2,1)} %convolution_convert_fusion.7.grad), channel_id=1, source_target_pairs={{0,2},{1,3},{2,4},{3,5},{4,6},{5,7},{8,10},{9,11},{10,12},{11,13},... | collective-permute-start | bytes 2359304 | tf_op jit(solution)/shard_map/ppermute | solution.py:814
  220.3 4.8 %copy-start.30 = (bf16[512,3072]{1,0:T(8,128)(2,1)S(1)}, bf16[512,3072]{1,0:T(8,128)(2,1)}, u32[]{:S(2)}) copy-start(bf16[512,3072]{1,0:T(8,128)(2,1)} %copy-done.29) | copy-start | bytes 9437188
  231.3 18.4 %copy-start.6 = (bf16[512,768]{1,0:T(8,128)(2,1)S(1)}, bf16[512,768]{1,0:T(8,128)(2,1)}, u32[]{:S(2)}) copy-start(bf16[512,768]{1,0:T(8,128)(2,1)} %refs_0_.1) | copy-start | bytes 2359300
  254.9 11.5 %copy-start.13 = (f32[12,1,512]{2,1,0:T(1,128)S(1)}, f32[12,1,512]{2,1,0:T(1,128)}, u32[]{:S(2)}) copy-start(f32[12,1,512]{2,1,0:T(1,128)} %get-tuple-element.46.logsum) | copy-start | bytes 73732
  259.8 32.1 %collective-permute-start.1 = (bf16[512,768]{1,0:T(8,128)(2,1)}, bf16[512,768]{1,0:T(8,128)(2,1)S(1)}, u32[]{:S(2)}, u32[]{:S(2)}) collective-permute-start(bf16[512,768]{1,0:T(8,128)(2,1)} %convolution_convert_fusion.7.grad), channel_id=1, source_target_pairs={{0,1},{1,2},{2,3},{3,4},{4,5},{5,6},{6,7},{8,9},{9,10},{10,11},{11... | collective-permute-start | bytes 2359304 | tf_op jit(solution)/shard_map/ppermute | solution.py:814
  265.1 28.0 %collective-permute-start.2 = (bf16[512,768]{1,0:T(8,128)(2,1)}, bf16[512,768]{1,0:T(8,128)(2,1)S(1)}, u32[]{:S(2)}, u32[]{:S(2)}) collective-permute-start(bf16[512,768]{1,0:T(8,128)(2,1)} %convolution_convert_fusion.7.grad), channel_id=1, source_target_pairs={{1,0},{2,1},{3,2},{4,3},{5,4},{6,5},{7,6},{9,8},{10,9},{11,10},{12... | collective-permute-start | bytes 2359304 | tf_op jit(solution)/shard_map/ppermute | solution.py:814
  266.5 30.0 %collective-permute-start.3 = (bf16[512,768]{1,0:T(8,128)(2,1)}, bf16[512,768]{1,0:T(8,128)(2,1)S(1)}, u32[]{:S(2)}, u32[]{:S(2)}) collective-permute-start(bf16[512,768]{1,0:T(8,128)(2,1)} %convolution_convert_fusion.7.grad), channel_id=1, source_target_pairs={{2,0},{3,1},{4,2},{5,3},{6,4},{7,5},{10,8},{11,9},{12,10},{13,11},... | collective-permute-start | bytes 2359304 | tf_op jit(solution)/shard_map/ppermute | solution.py:814
  332.8 101.8 %copy-start.26 = (bf16[512,768]{1,0:T(8,128)(2,1)S(1)}, bf16[512,768]{1,0:T(8,128)(2,1)}, u32[]{:S(2)}) copy-start(bf16[512,768]{1,0:T(8,128)(2,1)} %get-tuple-element.48) | copy-start | bytes 2359300
  437.0 5.4 %copy-start.8 = (f32[96,768]{1,0:T(8,128)S(1)}, f32[96,768]{1,0:T(8,128)}, u32[]{:S(2)}) copy-start(f32[96,768]{1,0:T(8,128)} %get-tuple-element.137) | copy-start | bytes 884740
  (17 other events, 47.0 us)
